TPU v7x, 32 devices: a whole 2x2x4 slice. The times are simulated.
32 devices in a mesh: ctx: 4 (over z), fsdp: 8 (over y, x, core).
Axes of the slice: x: 2, y: 2, z: 4, core: 2. Of those that a mesh axis runs over, the one named last changes fastest.
Arguments:
- tokens: bfloat16 [8, 512, 1024], P('fsdp', 'ctx'), may hold values from -12 to 12
- cotangent: bfloat16 [8, 512, 1024], P('fsdp', 'ctx'), may hold values from -6 to 6
- weight_rows: float32 [12288, 1024], P('fsdp'), may hold values from -2 to 2
- first_rows: float32 [12288, 1024], P('fsdp')
- second_rows: float32 [12288, 1024], P('fsdp'), as said below
- vector_rows: float32 [12, 1024], replicated, may hold values from -2 to 2
- vector_first: float32 [12, 1024], replicated
- vector_second: float32 [12, 1024], replicated, as said below
Outputs:
- output: bfloat16 [8, 512, 1024], P('fsdp', 'ctx')
- input_grad: float32 [8, 512, 1024], P('fsdp', 'ctx')
- weight_grad: float32 [12288, 1024], P('fsdp')
- new_weights: float32 [12288, 1024], P('fsdp')
- new_first: float32 [12288, 1024], P('fsdp')
- new_second: float32 [12288, 1024], P('fsdp')
- vector_grad: float32 [12, 1024], replicated
- new_vectors: float32 [12, 1024], replicated
- new_vector_first: float32 [12, 1024], replicated
- new_vector_second: float32 [12, 1024], replicated
Inputs may be any that keep to these rules, and one draw needn't show every extreme that they name: `second_rows`: every entry is positive. `vector_second`: every entry is positive.
All inputs are finite; a program needn't handle non-finite values.
Results may differ from a plain program's by a relative error of at most 0.025.
The roundings to bfloat16 on the way count: a program that leaves them out, or rounds other values in their place, can miss the bound.
Values may be sent and summed in bfloat16 or wider, within the bound.
No kernel may reach another device: no remote copies, remote signals or barrier semaphores. Data moves between devices by JAX's collectives and lax.ppermute only.
A program may use at most 320 MiB of HBM per device.

v0:
```python
import math

import jax
import jax.numpy as jnp
from jax import lax
from jax.sharding import PartitionSpec as P

D = 1024
HEADS = 16


beta_one = 0.9
beta_two = 0.999
learn_rate = 0.01
decay_rate = 0.01
adam_eps = 1e-08
norm_eps = 1e-05
adam_step = 2


def mat_nt(left, right):
    return lax.dot_general(
        left, right, (((1,), (1,)), ((), ())), preferred_element_type=jnp.float32
    )


def mat_tn(left, right):
    return lax.dot_general(
        left, right, (((0,), (0,)), ((), ())), preferred_element_type=jnp.float32
    )


def unpack(rows, vectors):
    width = rows.shape[1]
    hidden = (rows.shape[0] - 4 * width) // 2
    return [
        rows[: 3 * width],
        vectors[0],
        vectors[1],
        rows[3 * width : 4 * width],
        vectors[2],
        vectors[3],
        vectors[4],
        rows[4 * width : 4 * width + hidden],
        vectors[8:].reshape(hidden),
        rows[4 * width + hidden :],
        vectors[5],
        vectors[6],
        vectors[7],
    ]


def normalize(values):
    centred = values - jnp.mean(values, axis=-1, keepdims=True)
    inverse = lax.rsqrt(jnp.mean(centred * centred, axis=-1, keepdims=True) + norm_eps)
    return (centred * inverse, inverse)


def norm_back(grad_norm, normed, inverse):
    return inverse * (
        grad_norm
        - jnp.mean(grad_norm, axis=-1, keepdims=True)
        - normed * jnp.mean(grad_norm * normed, axis=-1, keepdims=True)
    )


def gelu_grad(pre_act):
    return (
        0.5 * (1.0 + lax.erf(pre_act * 0.7071067811865476))
        + pre_act * jnp.exp(-0.5 * pre_act * pre_act) * 0.3989422804014327
    )


def project(inputs, params):
    qkv_t, query_b, value_b = (params[0], params[1], params[2])
    width = qkv_t.shape[1]
    projected = mat_nt(inputs, qkv_t)
    query_rows = (projected[:, :width] + query_b.astype(jnp.float32)).astype(jnp.bfloat16)
    key_rows = projected[:, width : 2 * width].astype(jnp.bfloat16)
    value_rows = (projected[:, 2 * width :] + value_b.astype(jnp.float32)).astype(jnp.bfloat16)
    return (query_rows, key_rows, value_rows)


def tail_forward(inputs, attended, params):
    out_t, out_b, gain_one, shift_one, up_t, up_b, down_w, down_b, gain_two, shift_two = params[3:]
    first_sum = inputs.astype(jnp.float32) + mat_nt(attended, out_t) + out_b.astype(jnp.float32)
    normed_one, inverse_one = normalize(first_sum)
    hidden_in = normed_one * gain_one.astype(jnp.float32) + shift_one.astype(jnp.float32)
    hidden_b = hidden_in.astype(jnp.bfloat16)
    pre_act = mat_nt(hidden_b, up_t) + up_b.astype(jnp.float32)
    activ_b = jax.nn.gelu(pre_act, approximate=False).astype(jnp.bfloat16)
    second_sum = (
        hidden_in
        + jnp.dot(activ_b, down_w, preferred_element_type=jnp.float32)
        + down_b.astype(jnp.float32)
    )
    normed_two, inverse_two = normalize(second_sum)
    output = (normed_two * gain_two.astype(jnp.float32) + shift_two.astype(jnp.float32)).astype(
        jnp.bfloat16
    )
    return (output, (normed_one, inverse_one, hidden_b, pre_act, activ_b, normed_two, inverse_two))


def tail_backward(cotan, attended, saved, params):
    out_t, out_b, gain_one, shift_one, up_t, up_b, down_w, down_b, gain_two, shift_two = params[3:]
    normed_one, inverse_one, hidden_b, pre_act, activ_b, normed_two, inverse_two = saved
    grad_gain_two = jnp.sum(cotan * normed_two, axis=0)
    grad_shift_two = jnp.sum(cotan, axis=0)
    grad_second = norm_back(cotan * gain_two.astype(jnp.float32), normed_two, inverse_two)
    grad_second_b = grad_second.astype(jnp.bfloat16)
    grad_down_b = jnp.sum(grad_second, axis=0)
    grad_down_w = mat_tn(activ_b, grad_second_b)
    grad_pre = mat_nt(grad_second_b, down_w) * gelu_grad(pre_act)
    grad_pre_b = grad_pre.astype(jnp.bfloat16)
    grad_up_b = jnp.sum(grad_pre, axis=0)
    grad_up_t = mat_tn(grad_pre_b, hidden_b)
    grad_hidden = grad_second + jnp.dot(grad_pre_b, up_t, preferred_element_type=jnp.float32)
    grad_gain_one = jnp.sum(grad_hidden * normed_one, axis=0)
    grad_shift_one = jnp.sum(grad_hidden, axis=0)
    grad_first = norm_back(grad_hidden * gain_one.astype(jnp.float32), normed_one, inverse_one)
    grad_first_b = grad_first.astype(jnp.bfloat16)
    grad_out_b = jnp.sum(grad_first, axis=0)
    grad_out_t = mat_tn(grad_first_b, attended)
    grad_attended = jnp.dot(grad_first_b, out_t, preferred_element_type=jnp.float32).astype(
        jnp.bfloat16
    )
    tail_grads = (
        grad_out_t,
        grad_out_b,
        grad_gain_one,
        grad_shift_one,
        grad_up_t,
        grad_up_b,
        grad_down_w,
        grad_down_b,
        grad_gain_two,
        grad_shift_two,
    )
    return (grad_first, grad_attended, tail_grads)


def head_backward(inputs, grad_first, grad_query, grad_key, grad_value, qkv_t):
    grad_proj_b = jnp.concatenate([grad_query, grad_key, grad_value], axis=1).astype(jnp.bfloat16)
    grad_qkv_t = mat_tn(grad_proj_b, inputs)
    grad_inputs = grad_first + jnp.dot(grad_proj_b, qkv_t, preferred_element_type=jnp.float32)
    return (grad_inputs, grad_qkv_t, jnp.sum(grad_query, axis=0), jnp.sum(grad_value, axis=0))


def pack_grads(grad_qkv_t, grad_query_b, grad_value_b, tail_grads):
    width = grad_qkv_t.shape[1]
    matrix = jnp.concatenate([grad_qkv_t, tail_grads[0], tail_grads[4], tail_grads[6]], axis=0)
    small = jnp.stack(
        [
            grad_query_b,
            grad_value_b,
            tail_grads[1],
            tail_grads[2],
            tail_grads[3],
            tail_grads[7],
            tail_grads[8],
            tail_grads[9],
        ]
    )
    vectors = jnp.concatenate([small, tail_grads[5].reshape(-1, width)], axis=0)
    return (matrix, vectors)


def adam_update(weights, grads, first, second):
    first_new = beta_one * first + (1.0 - beta_one) * grads
    second_new = beta_two * second + (1.0 - beta_two) * grads * grads
    first_hat = first_new / (1.0 - beta_one**adam_step)
    second_hat = second_new / (1.0 - beta_two**adam_step)
    weights_new = weights - learn_rate * (
        first_hat / (jnp.sqrt(second_hat) + adam_eps) + decay_rate * weights
    )
    return (weights_new, first_new, second_new)


def split_heads(matrix):
    return matrix.reshape(matrix.shape[0], HEADS, matrix.shape[1] // HEADS)


def local(
    tokens,
    cotangent,
    weight_rows,
    first_rows,
    second_rows,
    vector_rows,
    vector_first,
    vector_second,
):
    row_count = tokens.shape[1]
    inputs = tokens.reshape(row_count, D)
    cotan = cotangent.reshape(row_count, D).astype(jnp.float32)
    head_width = D // HEADS
    score_scale = 1.0 / math.sqrt(head_width)
    vectors_b = vector_rows.astype(jnp.bfloat16)
    gathered = lax.all_gather(weight_rows.astype(jnp.bfloat16), "fsdp", axis=0, tiled=True)
    params = unpack(gathered, vectors_b)
    query_rows, key_rows, value_rows = project(inputs, params)
    query_heads = split_heads(query_rows)
    start_state = (
        jnp.full((HEADS, row_count), -jnp.inf, jnp.float32),
        jnp.zeros((HEADS, row_count), jnp.float32),
        jnp.zeros((HEADS, row_count, head_width), jnp.float32),
    )
    key_piece = lax.all_gather(key_rows, "ctx", axis=0, tiled=True)
    value_piece = lax.all_gather(value_rows, "ctx", axis=0, tiled=True)
    amount = key_piece.shape[0]
    block_rows = math.gcd(amount, 512)

    def one_block(position, running):
        row_top, row_total, weighted = running
        key_block = split_heads(
            lax.dynamic_slice_in_dim(key_piece, position * block_rows, block_rows, 0)
        )
        value_block = split_heads(
            lax.dynamic_slice_in_dim(value_piece, position * block_rows, block_rows, 0)
        ).astype(jnp.float32)
        scores = (
            jnp.einsum("qhd,khd->hqk", query_heads, key_block, preferred_element_type=jnp.float32)
            * score_scale
        )
        new_top = jnp.maximum(row_top, jnp.max(scores, axis=-1))
        rescale = jnp.exp(row_top - new_top)
        weights = jnp.exp(scores - new_top[:, :, None])
        row_total = row_total * rescale + jnp.sum(weights, axis=-1)
        weighted = weighted * rescale[:, :, None] + jnp.einsum(
            "hqk,khd->hqd", weights, value_block, precision=lax.Precision.HIGHEST
        )
        return (new_top, row_total, weighted)

    row_top, row_total, weighted = lax.fori_loop(0, amount // block_rows, one_block, start_state)
    attended = (
        (weighted / row_total[:, :, None])
        .transpose(1, 0, 2)
        .reshape(row_count, D)
        .astype(jnp.bfloat16)
    )
    log_totals = row_top + jnp.log(row_total)
    output, saved = tail_forward(inputs, attended, params)
    grad_first, grad_attended, tail_grads = tail_backward(cotan, attended, saved, params)
    grad_heads = split_heads(grad_attended)
    delta = jnp.sum(
        grad_heads.astype(jnp.float32) * split_heads(attended).astype(jnp.float32), axis=-1
    ).T
    seq_length = row_count * lax.axis_size("ctx")
    back_state = (
        jnp.zeros((row_count, HEADS, head_width), jnp.float32),
        jnp.zeros((seq_length, D), jnp.float32),
        jnp.zeros((seq_length, D), jnp.float32),
    )
    attend_key_piece = lax.all_gather(key_rows, "ctx", axis=0, tiled=True)
    attend_value_piece = lax.all_gather(value_rows, "ctx", axis=0, tiled=True)
    amount = attend_key_piece.shape[0]
    attend_block_rows = math.gcd(amount, 512)

    def one_block(position, running):
        grad_query, grad_key, grad_value = running
        offset = position * attend_block_rows
        key_block = split_heads(
            lax.dynamic_slice_in_dim(attend_key_piece, offset, attend_block_rows, 0)
        )
        value_block = split_heads(
            lax.dynamic_slice_in_dim(attend_value_piece, offset, attend_block_rows, 0)
        )
        scores = (
            jnp.einsum("qhd,khd->hqk", query_heads, key_block, preferred_element_type=jnp.float32)
            * score_scale
        )
        probs = jnp.exp(scores - log_totals[:, :, None])
        grad_probs = jnp.einsum(
            "qhd,khd->hqk", grad_heads, value_block, preferred_element_type=jnp.float32
        )
        grad_scores = (probs * (grad_probs - delta[:, :, None])).astype(jnp.bfloat16)
        grad_query = (
            grad_query
            + jnp.einsum("hqk,khd->qhd", grad_scores, key_block, preferred_element_type=jnp.float32)
            * score_scale
        )
        key_term = (
            jnp.einsum("hqk,qhd->khd", grad_scores, query_heads, preferred_element_type=jnp.float32)
            * score_scale
        )
        value_term = jnp.einsum(
            "hqk,qhd->khd",
            probs.astype(jnp.bfloat16),
            grad_heads,
            preferred_element_type=jnp.float32,
        )
        grad_key = lax.dynamic_update_slice_in_dim(
            grad_key, key_term.reshape(attend_block_rows, D), offset, 0
        )
        grad_value = lax.dynamic_update_slice_in_dim(
            grad_value, value_term.reshape(attend_block_rows, D), offset, 0
        )
        return (grad_query, grad_key, grad_value)

    grad_query, grad_key_all, grad_value_all = lax.fori_loop(
        0, amount // attend_block_rows, one_block, back_state
    )
    grad_key, grad_value = (
        lax.psum_scatter(
            grad_key_all.astype(jnp.bfloat16), "ctx", scatter_dimension=0, tiled=True
        ).astype(jnp.float32),
        lax.psum_scatter(
            grad_value_all.astype(jnp.bfloat16), "ctx", scatter_dimension=0, tiled=True
        ).astype(jnp.float32),
    )
    grad_query = grad_query.reshape(row_count, D)
    grad_inputs, grad_qkv_t, grad_query_b, grad_value_b = head_backward(
        inputs, grad_first, grad_query, grad_key, grad_value, params[0]
    )
    matrix, vectors = pack_grads(grad_qkv_t, grad_query_b, grad_value_b, tail_grads)
    vector_total = lax.psum(vectors, ("ctx", "fsdp"))
    new_vectors, new_vfirst, new_vsecond = adam_update(
        vector_rows, vector_total, vector_first, vector_second
    )
    grads = lax.psum_scatter(matrix.astype(jnp.bfloat16), "fsdp", scatter_dimension=0, tiled=True)
    grad_out = lax.psum(grads, "ctx").astype(jnp.float32)
    weights_out, first_out, second_out = adam_update(weight_rows, grad_out, first_rows, second_rows)
    return (
        output.reshape(1, row_count, D),
        grad_inputs.reshape(1, row_count, D),
        grad_out,
        weights_out,
        first_out,
        second_out,
        vector_total,
        new_vectors,
        new_vfirst,
        new_vsecond,
    )


def solution(mesh):
    return jax.shard_map(
        local,
        mesh=mesh,
        in_specs=(
            P("fsdp", "ctx", None),
            P("fsdp", "ctx", None),
            P("fsdp", None),
            P("fsdp", None),
            P("fsdp", None),
            P(),
            P(),
            P(),
        ),
        out_specs=(
            P("fsdp", "ctx", None),
            P("fsdp", "ctx", None),
            P("fsdp", None),
            P("fsdp", None),
            P("fsdp", None),
            P("fsdp", None),
            P(),
            P(),
            P(),
            P(),
        ),
        check_vma=False,
    )
```

profile of v0, /device:TPU:14, one launch (start us, length us, event | category | flops | bytes accessed | tf_op | source)
XLA Modules:
  0.0 667.6 jit_solution(5482531895368750081)
XLA Ops:
  7.2 5.0 convert_element_type.122
  12.3 125.5 %all-gather.4.cloned.1.call-done = bf16[12288,1024]{1,0:T(8,128)(2,1)} async-done(((bf16[1536,1024]{1,0:T(8,128)(2,1)}), bf16[12288,1024]{1,0:T(8,128)(2,1)}) %all-gather.4.cloned.1.call-update) | async-done | bytes 25165840 | tf_op jit(solution)/shard_map/all_gather | solution.py:199
  137.7 5.0 fusion.11
  144.7 27.8 %all-gather.6.cloned.1.call-done = bf16[512,1024]{1,0:T(8,128)(2,1)} async-done(((bf16[128,1024]{1,0:T(8,128)(2,1)}), bf16[512,1024]{1,0:T(8,128)(2,1)}) %all-gather.6.cloned.1.call-update) | async-done | bytes 1048592 | tf_op jit(solution)/shard_map/all_gather | solution.py:208
  172.5 1.5 copy.30
  176.9 25.2 %all-gather.8.cloned.1.call-done = bf16[512,1024]{1,0:T(8,128)(2,1)} async-done(((bf16[128,1024]{1,0:T(8,128)(2,1)}), bf16[512,1024]{1,0:T(8,128)(2,1)}) %all-gather.8.cloned.1.call-update) | async-done | bytes 1048592 | tf_op jit(solution)/shard_map/all_gather | solution.py:209
  202.0 1.5 copy.31
  203.5 5.7 fusion.78
  209.3 2.6 fusion.114
  212.1 9.4 %fusion.25 = (bf16[128,4096]{1,0:T(8,128)(2,1)S(1)}, f32[128,4096]{1,0:T(8,128)S(1)}) fusion(f32[4096]{0:T(1024)S(1)} %bitcast.132, bf16[12288,1024]{1,0:T(8,128)(2,1)} %all-gather.4.cloned.1.call-done, f32[128,1024]{1,0:T(8,128)S(1)} %get-tuple-element.103, f32[1024]{0:T(1024)S(1)} %bitcast.121, f32[1024]{0:T(1024)S(1)} %bitcast.113, ...), kind=kOutput, calls=%fused_computation.34 | convolution fusion | flops 1109000192 | bytes 12084224 | tf_op jit(solution)/shard_map/dot_general | solution.py:22
  221.5 5.3 fusion.115
  228.3 6.7 fusion.116
  235.0 5.3 multiply_reduce_fusion.1
  241.3 2.0 fusion.74
  243.5 3.2 fusion.47
  246.7 1.3 copy.35
  248.2 3.9 multiply_convert_fusion
  252.1 1.4 multiply_convert_fusion.1
  253.5 2.3 copy.33
  256.1 3.1 convolution_convert_fusion.3
  259.2 1.5 fusion.113
  260.8 5.6 convolution_convert_fusion
  266.4 5.6 convolution_convert_fusion.1
  273.9 27.4 %reduce-scatter.10.cloned.1.call-done = bf16[128,1024]{1,0:T(8,128)(2,1)} async-done(((bf16[512,1024]{1,0:T(8,128)(2,1)}), bf16[128,1024]{1,0:T(8,128)(2,1)}) %reduce-scatter.10.cloned.1.call-update) | async-done | bytes 262160
  301.4 1.8 copy.34
  303.2 2.9 convolution_convert_fusion.2
  306.1 59.3 %pad_maximum_fusion = bf16[12288,1024]{1,0:T(8,128)(2,1)} fusion(bf16[4096,1024]{1,0:T(8,128)(2,1)} %convolution_convert_fusion, bf16[4096,1024]{1,0:T(8,128)(2,1)} %convolution_convert_fusion.1, bf16[1024,1024]{1,0:T(8,128)(2,1)} %convolution_convert_fusion.3, bf16[3072,1024]{1,0:T(8,128)(2,1)S(1)} %convolution_convert_fusion.2), kind=kLoop, calls=%fused_computation | loop fusion | flops 100663296 | bytes 50331648 | tf_op jit(solution)/shard_map/concatenate | solution.py:151
  365.5 156.0 %reduce-scatter.8.cloned.1.call-done = bf16[1536,1024]{1,0:T(8,128)(2,1)} async-done(((bf16[12288,1024]{1,0:T(8,128)(2,1)}), bf16[1536,1024]{1,0:T(8,128)(2,1)}) %reduce-scatter.8.cloned.1.call-update) | async-done | bytes 3145744 | tf_op jit(solution)/shard_map/reduce_scatter | solution.py:320
  521.9 44.1 %psum.15 = f32[12,1024]{1,0:T(8,128)S(1)} all-reduce(f32[12,1024]{1,0:T(8,128)S(1)} %concatenate.13), channel_id=1, replica_groups=mesh['ctx'=4,'fsdp'=8] {'ctx','fsdp'}, use_global_device_ids=true, to_apply=%region_24.0 | all-reduce | flops 12288 | bytes 98304 | tf_op jit(solution)/shard_map/psum | solution.py:316
  566.8 4.6 fusion.71
  571.4 73.6 %all-reduce.2.cloned.1.call-done = bf16[1536,1024]{1,0:T(8,128)(2,1)} async-done(((bf16[1536,1024]{1,0:T(8,128)(2,1)}), bf16[1536,1024]{1,0:T(8,128)(2,1)}) %all-reduce.2.cloned.1.call-update) | async-done | bytes 3145744 | tf_op jit(solution)/shard_map/psum | solution.py:321
  645.0 15.3 %multiply_subtract_fusion = (f32[1536,1024]{1,0:T(8,128)}, f32[1536,1024]{1,0:T(8,128)}, f32[1536,1024]{1,0:T(8,128)}, f32[1536,1024]{1,0:T(8,128)}) fusion(f32[1536,1024]{1,0:T(8,128)} %param.10, f32[1536,1024]{1,0:T(8,128)} %param.11, f32[1536,1024]{1,0:T(8,128)} %param.12, bf16[1536,1024]{1,0:T(8,128)(2,1)} %all-reduce.2.cloned.1.call-done), kind=kLoop, calls=%fused_computation.13 | loop fusion | flops 25165824 | bytes 47185920 | tf_op jit(solution)/shard_map/sub | solution.py:173
  (97 shorter events, 11.3 us)
Async XLA Ops:
  7.2 130.5 %all-gather.4.cloned.1.call-start = ((), (), s32[]{:S(2)}) async-start(), calls=%async_computation.3 | async-start | bytes 28311552 | tf_op jit(solution)/shard_map/all_gather | solution.py:199
  12.2 125.5 %copy-start.20 = (bf16[1,128,1024]{2,1,0:T(8,128)(2,1)S(1)}, bf16[1,128,1024]{2,1,0:T(8,128)(2,1)}, u32[]{:S(2)}) copy-start(bf16[1,128,1024]{2,1,0:T(8,128)(2,1)} %param.8) | copy-start | bytes 786436
  12.2 131.3 %copy-start.21 = (f32[12,1024]{1,0:T(8,128)S(1)}, f32[12,1024]{1,0:T(8,128)}, u32[]{:S(2)}) copy-start(f32[12,1024]{1,0:T(8,128)} %param.13) | copy-start | bytes 147460
  12.2 160.3 %all-gather.6.cloned.1.call-start = ((), (), s32[]{:S(2)}) async-start(), calls=%async_computation.4 | async-start | bytes 1310720 | tf_op jit(solution)/shard_map/all_gather | solution.py:208
  143.4 58.6 %all-gather.8.cloned.1.call-start = ((), (), s32[]{:S(2)}) async-start(), calls=%async_computation.5 | async-start | bytes 1310720 | tf_op jit(solution)/shard_map/all_gather | solution.py:209
  144.4 128.4 %reduce-scatter.12.cloned.1.call-start = ((), (), s32[]{:S(2)}) async-start(), calls=%async_computation.9 | async-start | bytes 1310720
  144.6 30.2 %copy-start.10 = (bf16[128,1024]{0,1:T(8,128)(2,1)}, bf16[128,1024]{0,1:T(8,128)(2,1)S(1)}, u32[]{:S(2)}) copy-start(bf16[128,1024]{0,1:T(8,128)(2,1)S(1)} %copy.29) | copy-start | bytes 786436
  174.8 2.0 copy-start
  203.5 5.7 copy-start.3
  209.2 38.9 %copy-start.18 = (bf16[128,16,64]{0,2,1:T(8,128)(2,1)}, bf16[128,16,64]{0,2,1:T(8,128)(2,1)S(1)}, u32[]{:S(2)}) copy-start(bf16[128,16,64]{0,2,1:T(8,128)(2,1)S(1)} %fusion.78) | copy-start | bytes 786436
  211.9 28.4 %copy-start.1 = (f32[128,1024]{1,0:T(8,128)}, f32[128,1024]{1,0:T(8,128)S(1)}, u32[]{:S(2)}) copy-start(f32[128,1024]{1,0:T(8,128)S(1)} %get-tuple-element.103) | copy-start | bytes 1572868
  221.5 5.3 copy-start.4
  221.5 5.5 copy-start.8
  228.3 6.7 %copy-start.12 = (f32[128,1024]{1,0:T(8,128)}, f32[128,1024]{1,0:T(8,128)S(1)}, u32[]{:S(2)}) copy-start(f32[128,1024]{1,0:T(8,128)S(1)} %get-tuple-element.78) | copy-start | bytes 1572868
  234.9 5.3 copy-start.6
  240.5 0.8 copy-start.14
  248.0 53.3 %reduce-scatter.10.cloned.1.call-start = ((), (), s32[]{:S(2)}) async-start(), calls=%async_computation.8 | async-start | bytes 1310720
  248.2 3.9 copy-start.11
  253.5 2.6 copy-start.19
  255.9 265.6 %reduce-scatter.8.cloned.1.call-start = ((), (), s32[]{:S(2)}) async-start(), calls=%async_computation.6 | async-start | bytes 28311552 | tf_op jit(solution)/shard_map/reduce_scatter | solution.py:320
  259.2 1.5 copy-start.5
  259.2 1.5 copy-start.13
  260.8 5.6 copy-start.2
  260.8 5.6 copy-start.7
  365.4 156.1 %copy-start.9 = (bf16[1,128,1024]{2,1,0:T(8,128)(2,1)S(1)}, bf16[1,128,1024]{2,1,0:T(8,128)(2,1)}, u32[]{:S(2)}) copy-start(bf16[1,128,1024]{2,1,0:T(8,128)(2,1)} %param.9) | copy-start | bytes 786436
  365.4 200.6 %copy-start.23 = (f32[12,1024]{1,0:T(8,128)S(1)}, f32[12,1024]{1,0:T(8,128)}, u32[]{:S(2)}) copy-start(f32[12,1024]{1,0:T(8,128)} %param.14) | copy-start | bytes 147460
  365.4 200.6 %copy-start.24 = (f32[12,1024]{1,0:T(8,128)S(1)}, f32[12,1024]{1,0:T(8,128)}, u32[]{:S(2)}) copy-start(f32[12,1024]{1,0:T(8,128)} %param.15) | copy-start | bytes 147460
  365.4 279.6 %all-reduce.2.cloned.1.call-start = ((), (), s32[]{:S(2)}) async-start(), calls=%async_computation.7 | async-start | bytes 6291456 | tf_op jit(solution)/shard_map/psum | solution.py:321
  521.5 45.2 %copy-start.15 = (f32[128,1024]{1,0:T(8,128)S(1)}, f32[128,1024]{1,0:T(8,128)}, u32[]{:S(2)}) copy-start(f32[128,1024]{1,0:T(8,128)} %copy-done.14) | copy-start | bytes 1572868
  521.5 45.2 %copy-start.16 = (bf16[128,1024]{0,1:T(8,128)(2,1)S(1)}, bf16[128,1024]{0,1:T(8,128)(2,1)}, u32[]{:S(2)}) copy-start(bf16[128,1024]{0,1:T(8,128)(2,1)} %copy.34) | copy-start | bytes 786436
  521.5 45.2 %copy-start.17 = (bf16[128,16,64]{0,2,1:T(8,128)(2,1)S(1)}, bf16[128,16,64]{0,2,1:T(8,128)(2,1)}, u32[]{:S(2)}) copy-start(bf16[128,16,64]{0,2,1:T(8,128)(2,1)} %get-tuple-element.89) | copy-start | bytes 786436
  566.0 5.3 copy-start.22
Sparse Core Ops, SparseCore 0:
  12.3 125.3 all-gather.3
  143.6 28.8 all-gather.5
  174.6 27.3 all-gather.7
  248.2 24.6 reduce-scatter.11
  275.5 25.7 reduce-scatter.9
  365.5 155.9 reduce-scatter.7
  523.9 121.0 all-reduce.1
where the time goes:
time: 679 us; the launch traced here: 668 us
  waiting for transfers between devices  436 us (64%)
  other arithmetic  84.5 us (12%)
  matrix products  74.6 us (11%)
  blocking collectives  44.1 us (6%)
  between operations  15 us (2%)
  local copies, waits for them, and re-layouts  12.5 us (2%)
    reduce_scatter x1, waiting for transfers between devices, local(): lax.psum_scatter(matrix.astype(jnp.bfloat16), 'fsdp', scatter_dimension=0...  156 us
    all_gather x1, waiting for transfers between devices, local(): lax.all_gather(weight_rows.astype(jnp.bfloat16), 'fsdp', axis=0, tiled=True)  125 us
    psum x1, waiting for transfers between devices, local(): grad_out = lax.psum(grads, 'ctx').astype(jnp.float32)  73.6 us
    concatenate x1, other arithmetic, pack_grads(): jnp.concatenate([grad_qkv_t, tail_grads[0], tail_grads[4], tail_grads[6]]...  59.3 us
    psum x1, blocking collectives, local(): vector_total = lax.psum(vectors, ('ctx', 'fsdp'))  44.1 us
    unnamed x9, waiting for transfers between devices  28.4 us
    all_gather x1, waiting for transfers between devices, local(): key_piece = lax.all_gather(key_rows, 'ctx', axis=0, tiled=True)  27.8 us
    all_gather x1, waiting for transfers between devices, local(): value_piece = lax.all_gather(value_rows, 'ctx', axis=0, tiled=True)  25.2 us
  transfers between devices with their start and end apart: 7, of which 7 were waited for; matrix products, arithmetic and copies ran while one was open for 5% of the time, Pallas kernels for 0%

commit v1 on v0

v1 whole, which is shorter than its diff:
```python
import math

import jax
import jax.numpy as jnp
from jax import lax
from jax.sharding import PartitionSpec as P

D = 1024
HEADS = 16
HEAD_DIM = D // HEADS

beta_one = 0.9
beta_two = 0.999
learn_rate = 0.01
decay_rate = 0.01
adam_eps = 1e-08
norm_eps = 1e-05
adam_step = 2

f32 = jnp.float32
bf16 = jnp.bfloat16


def mat_nt(left, right):
    return lax.dot_general(left, right, (((1,), (1,)), ((), ())), preferred_element_type=f32)


def mat_tn(left, right):
    return lax.dot_general(left, right, (((0,), (0,)), ((), ())), preferred_element_type=f32)


def mat_nn(left, right):
    return jnp.dot(left, right, preferred_element_type=f32)


def normalize(values):
    centred = values - jnp.mean(values, axis=-1, keepdims=True)
    inverse = lax.rsqrt(jnp.mean(centred * centred, axis=-1, keepdims=True) + norm_eps)
    return (centred * inverse, inverse)


def norm_back(grad_norm, normed, inverse):
    return inverse * (
        grad_norm
        - jnp.mean(grad_norm, axis=-1, keepdims=True)
        - normed * jnp.mean(grad_norm * normed, axis=-1, keepdims=True)
    )


def adam_update(weights, grads, first, second):
    first_new = beta_one * first + (1.0 - beta_one) * grads
    second_new = beta_two * second + (1.0 - beta_two) * grads * grads
    first_hat = first_new / (1.0 - beta_one**adam_step)
    second_hat = second_new / (1.0 - beta_two**adam_step)
    weights_new = weights - learn_rate * (
        first_hat / (jnp.sqrt(second_hat) + adam_eps) + decay_rate * weights
    )
    return (weights_new, first_new, second_new)


def at(array, index, axis=0):
    return lax.dynamic_index_in_dim(array, index, axis, keepdims=False)


def local(
    tokens,
    cotangent,
    weight_rows,
    first_rows,
    second_rows,
    vector_rows,
    vector_first,
    vector_second,
):
    C = lax.axis_size("ctx")
    F = lax.axis_size("fsdp")
    K = F // C
    z = lax.axis_index("ctx")
    f = lax.axis_index("fsdp")
    g = f // K
    c = f % K
    T = tokens.shape[1]
    own_rows = weight_rows.shape[0]
    total_rows = own_rows * F
    hidden = (total_rows - 4 * D) // 2
    B = math.gcd(own_rows, D)
    direct = (B // C) % HEAD_DIM == 0
    if not direct:
        B = D
    s = B // C
    per = D // B
    nb = own_rows // B if direct else 0
    blocks = total_rows // B
    first_o, last_o = 3 * per, 4 * per

    swap_pairs = [
        (zz * F + K * gg + cc, gg * F + K * zz + cc)
        for zz in range(C)
        for gg in range(C)
        for cc in range(K)
    ]

    def swap(array):
        return lax.ppermute(array, ("ctx", "fsdp"), swap_pairs)

    def hop(array, d):
        return lax.ppermute(array, "fsdp", [(i, K * ((i // K) ^ d) + i % K) for i in range(F)])

    def gather(block):
        return jnp.concatenate([block] + [hop(block, d) for d in range(1, C)], axis=0)

    def scatter(partial):
        parts = partial.reshape(C, T, D)
        sent = parts.astype(bf16)
        total = parts[0]
        for d in range(1, C):
            total = total + hop(sent[d], d).astype(f32)
        return total

    def cores(array, k):
        return lax.ppermute(array, "fsdp", [(i, K * (i // K) + (i + k) % K) for i in range(F)])

    ring_pairs = [(i, (i + 1) % C) for i in range(C)]

    def ring_scatter(parts):
        total = at(parts, (z + C - 1) % C)
        for step in range(C - 1):
            arrived = lax.ppermute(total.astype(bf16), "ctx", ring_pairs)
            total = arrived.astype(f32) + at(parts, (z + 2 * C - 2 - step) % C)
        return total

    def ring_gather(block):
        held = [block]
        for _ in range(C - 1):
            held.append(lax.ppermute(held[-1], "ctx", ring_pairs))
        held = jnp.stack(held)
        return [at(held, (z + C - zz) % C) for zz in range(C)]

    def row_form(rows):
        return rows.reshape(-1, C, s, D)

    def column_form(rows):
        n = rows.shape[0] // B
        return rows.reshape(n, C, s, per, C, s).transpose(0, 4, 2, 1, 3, 5).reshape(n, C, s, D)

    def from_column_form(blocks_):
        n = blocks_.shape[0]
        return blocks_.reshape(n, C, s, C, per, s).transpose(0, 3, 2, 4, 1, 5).reshape(n, B, D)

    block_ids = nb * f + jnp.arange(max(nb, 1))
    is_o = ((block_ids >= first_o) & (block_ids < last_o))[:, None, None, None]

    weights_b = weight_rows.astype(bf16)
    if direct:
        payload = jnp.where(is_o, column_form(weights_b), row_form(weights_b))
        parts = [at(payload, g, 1)]
        for d in range(1, C):
            parts.append(hop(at(payload, g ^ d, 1), d))
        mine = jnp.stack(parts)
        both = jnp.stack([mine] + [cores(mine, k) for k in range(1, K)])
        slices = jnp.concatenate(
            [at(at(both, (c - cc) % K), gg ^ g) for gg in range(C) for cc in range(K)], axis=0
        )
    else:
        full = lax.all_gather(weights_b, "fsdp", axis=0, tiled=True)
        rows_part = at(row_form(full), g, 1)
        cols_part = at(column_form(full), g, 1)
        slices = jnp.concatenate(
            [rows_part[:first_o], cols_part[first_o:last_o], rows_part[last_o:]], axis=0
        )
    part = D // C
    w_qkv = slices[:first_o].reshape(3 * part, D)
    w_o = (
        slices[first_o:last_o]
        .reshape(per, s, C, per, s)
        .transpose(0, 2, 1, 3, 4)
        .reshape(D, part)
    )
    up_end = last_o + hidden // B
    w_1 = slices[last_o:up_end].reshape(hidden // C, D)
    w_2 = slices[up_end:].reshape(hidden // C, D)

    vectors = vector_rows.astype(bf16).astype(f32)

    def own_features(vector):
        return at(vector.reshape(-1, C, s), g, 1).reshape(-1)

    def place_features(vector, count):
        spread = jnp.zeros((count // B, C, s), f32)
        return lax.dynamic_update_slice(
            spread, vector.reshape(count // B, 1, s), (0, g, 0)
        ).reshape(count)

    query_b, value_b = own_features(vectors[0]), own_features(vectors[1])
    out_b, gain_one, shift_one, down_b, gain_two, shift_two = [vectors[i] for i in range(2, 8)]
    up_b = own_features(vectors[8:].reshape(hidden))

    inputs = swap(tokens.reshape(T, D))
    cotan = swap(cotangent.reshape(T, D)).astype(f32)
    sequence = gather(inputs)
    S = C * T
    heads = part // HEAD_DIM
    score_scale = 1.0 / math.sqrt(HEAD_DIM)

    def split_heads(matrix):
        return matrix.reshape(S, heads, HEAD_DIM).transpose(1, 0, 2)

    def join_heads(stacked):
        return stacked.transpose(1, 0, 2).reshape(S, part)

    def batched(spec, left, right):
        return jnp.einsum(spec, left, right, preferred_element_type=f32)

    projected = mat_nt(sequence, w_qkv)
    query = split_heads((projected[:, :part] + query_b).astype(bf16))
    key = split_heads(projected[:, part : 2 * part].astype(bf16))
    value = split_heads((projected[:, 2 * part :] + value_b).astype(bf16))
    scores = batched("hqd,hkd->hqk", query, key) * score_scale
    top = jnp.max(scores, axis=-1, keepdims=True)
    log_total = top + jnp.log(jnp.sum(jnp.exp(scores - top), axis=-1, keepdims=True))
    probs = jnp.exp(scores - log_total)
    probs_b = probs.astype(bf16)
    attended_h = batched("hqk,hkd->hqd", probs_b, value).astype(bf16)
    attended = join_heads(attended_h)

    first_sum = inputs.astype(f32) + scatter(mat_nt(attended, w_o)) + out_b
    normed_one, inverse_one = normalize(first_sum)
    hidden_in = normed_one * gain_one + shift_one
    hidden_all = gather(hidden_in.astype(bf16))
    pre_act = mat_nt(hidden_all, w_1) + up_b
    cdf = 0.5 * (1.0 + lax.erf(pre_act * 0.7071067811865476))
    activ_b = (pre_act * cdf).astype(bf16)
    second_sum = hidden_in + scatter(mat_nn(activ_b, w_2)) + down_b
    normed_two, inverse_two = normalize(second_sum)
    output = swap((normed_two * gain_two + shift_two).astype(bf16))

    grad_gain_two = jnp.sum(cotan * normed_two, axis=0)
    grad_shift_two = jnp.sum(cotan, axis=0)
    grad_second = norm_back(cotan * gain_two, normed_two, inverse_two)
    grad_down_b = jnp.sum(grad_second, axis=0)
    grad_second_all = gather(grad_second.astype(bf16))
    grad_down_w = mat_tn(activ_b, grad_second_all)
    gelu_grad = cdf + pre_act * jnp.exp(-0.5 * pre_act * pre_act) * 0.3989422804014327
    grad_pre = mat_nt(grad_second_all, w_2) * gelu_grad
    grad_up_b = jnp.sum(grad_pre, axis=0)
    grad_pre_b = grad_pre.astype(bf16)
    grad_hidden = grad_second + scatter(mat_nn(grad_pre_b, w_1))
    grad_up_w = mat_tn(grad_pre_b, hidden_all)
    grad_gain_one = jnp.sum(grad_hidden * normed_one, axis=0)
    grad_shift_one = jnp.sum(grad_hidden, axis=0)
    grad_first = norm_back(grad_hidden * gain_one, normed_one, inverse_one)
    grad_out_b = jnp.sum(grad_first, axis=0)
    grad_first_all = gather(grad_first.astype(bf16))
    grad_out_w = mat_tn(grad_first_all, attended)
    grad_att = split_heads(mat_nn(grad_first_all, w_o).astype(bf16))

    delta = jnp.sum(grad_att.astype(f32) * attended_h.astype(f32), axis=-1, keepdims=True)
    grad_probs = batched("hqd,hkd->hqk", grad_att, value)
    grad_scores = (probs * (grad_probs - delta)).astype(bf16)
    grad_query = join_heads(batched("hqk,hkd->hqd", grad_scores, key) * score_scale)
    grad_key = join_heads(batched("hqk,hqd->hkd", grad_scores, query) * score_scale)
    grad_value = join_heads(batched("hqk,hqd->hkd", probs_b, grad_att))
    grad_proj = jnp.concatenate([grad_query, grad_key, grad_value], axis=1).astype(bf16)
    grad_qkv_w = mat_tn(grad_proj, sequence)
    grad_inputs = swap((grad_first + scatter(mat_nn(grad_proj, w_qkv))).astype(bf16))

    small = jnp.stack(
        [
            place_features(jnp.sum(grad_query, axis=0), D),
            place_features(jnp.sum(grad_value, axis=0), D),
            grad_out_b,
            grad_gain_one,
            grad_shift_one,
            grad_down_b,
            grad_gain_two,
            grad_shift_two,
        ]
    )
    vector_total = jnp.concatenate(
        [small, place_features(grad_up_b, hidden).reshape(-1, D)], axis=0
    )
    vector_total = lax.psum(vector_total, ("ctx", "fsdp"))
    new_vectors, new_vfirst, new_vsecond = adam_update(
        vector_rows, vector_total, vector_first, vector_second
    )

    grad_blocks = jnp.concatenate(
        [
            grad_qkv_w.astype(bf16).reshape(3 * per, s, D),
            grad_out_w.astype(bf16)
            .reshape(per, C, s, per, s)
            .transpose(0, 2, 1, 3, 4)
            .reshape(per, s, D),
            grad_up_w.astype(bf16).reshape(hidden // B, s, D),
            grad_down_w.astype(bf16).reshape(hidden // B, s, D),
        ],
        axis=0,
    )
    if direct:
        by_owner = grad_blocks.reshape(C, K, nb * s, D)
        total = at(by_owner, c, 1).astype(f32)
        for k in range(1, K):
            total = total + cores(at(by_owner, (c + k) % K, 1), k).astype(f32)
        parts = total.reshape(C, nb, C, s // C, D).transpose(2, 0, 1, 3, 4)
        reduced = ring_scatter(parts).astype(bf16)
        pieces = [at(reduced, g)]
        for d in range(1, C):
            pieces.append(hop(at(reduced, g ^ d), d))
        pieces = jnp.stack(pieces)
        ordered = jnp.stack([at(pieces, gg ^ g) for gg in range(C)], axis=1)
        ordered = jnp.stack(ring_gather(ordered), axis=2)
        ordered = ordered.reshape(nb, C, s, D)
        grad_out = jnp.where(
            is_o.reshape(-1, 1, 1), from_column_form(ordered), ordered.reshape(nb, B, D)
        ).reshape(own_rows, D)
    else:
        spread = lax.dynamic_update_slice(
            jnp.zeros((blocks, C, s, D), bf16), grad_blocks[:, None], (0, g, 0, 0)
        )
        matrix = jnp.where(
            ((jnp.arange(blocks) >= first_o) & (jnp.arange(blocks) < last_o))[:, None, None],
            from_column_form(spread),
            spread.reshape(blocks, B, D),
        ).reshape(total_rows, D)
        grad_out = lax.psum_scatter(matrix, "fsdp", scatter_dimension=0, tiled=True)
        grad_out = lax.psum(grad_out, "ctx")
    grad_out = grad_out.astype(f32)
    weights_out, first_out, second_out = adam_update(weight_rows, grad_out, first_rows, second_rows)
    return (
        output.reshape(1, T, D),
        grad_inputs.astype(f32).reshape(1, T, D),
        grad_out,
        weights_out,
        first_out,
        second_out,
        vector_total,
        new_vectors,
        new_vfirst,
        new_vsecond,
    )


def solution(mesh):
    shared = P()
    rows = P("fsdp", None)
    blocks = P("fsdp", "ctx", None)
    return jax.shard_map(
        local,
        mesh=mesh,
        in_specs=(blocks, blocks, rows, rows, rows, shared, shared, shared),
        out_specs=(blocks, blocks, rows, rows, rows, rows, shared, shared, shared, shared),
        check_vma=False,
    )
```

time: 679 us -> 504 us (0.74); the launches traced: 668 us -> 500 us
  waiting for transfers between devices: 436 us -> 225 us
  starting transfers between devices: 0.5 us -> 68.7 us
  local copies, waits for them, and re-layouts: 12.5 us -> 64.5 us
  matrix products: 74.6 us -> 29.8 us
  other arithmetic: 84.5 us -> 55.4 us
  between operations: 15 us -> 2.03 us
  blocking collectives: 44.1 us -> 54.8 us
    ppermute x0 -> x42, waiting for transfers between devices: none -> 225 us  [the longest x30 94.1 us: hop(): lax.ppermute(array, 'fsdp', [(i, K * (i // K ^ d) + i % K) for i in range...]
    all_gather x3 -> x0, waiting for transfers between devices: 178 us -> none  [the longest x1 125 us: local(): lax.all_gather(weight_rows.astype(jnp.bfloat16), 'fsdp', axis=0, tiled=True)]
    reduce_scatter x1 -> x0, waiting for transfers between devices: 156 us -> none  [local(): lax.psum_scatter(matrix.astype(jnp.bfloat16), 'fsdp', scatter_dimension=0...]
    psum x1 -> x0, waiting for transfers between devices: 73.6 us -> none  [local(): grad_out = lax.psum(grads, 'ctx').astype(jnp.float32)]
    ppermute x0 -> x42, starting transfers between devices: none -> 68.7 us  [the longest x30 40.3 us: hop(): lax.ppermute(array, 'fsdp', [(i, K * (i // K ^ d) + i % K) for i in range...]
    concatenate x1 -> x3, other arithmetic: 59.3 us -> 2.7 us  [the longest x2 1.79 us: local(): jnp.concatenate([at(at(both, (c - cc) % K), gg ^ g) for gg in range(C) fo...]
    unnamed x9 -> x0, waiting for transfers between devices: 28.4 us -> none
    dot_general x10, matrix products: 33.7 us -> 11.4 us  [the longest x6 7.32 us: batched(): return jnp.einsum(spec, left, right, preferred_element_type=f32)]
  transfers between devices with their start and end apart: 7 -> 42, of which waited for: 7 -> 26; matrix products, arithmetic and copies ran while one was open for 5% -> 6% of each run, Pallas kernels for 0% -> 0%
where the time goes in v1:
time: 504 us; the launch traced here: 500 us
  waiting for transfers between devices  225 us (45%)
  starting transfers between devices  68.7 us (14%)
  local copies, waits for them, and re-layouts  64.5 us (13%)
  other arithmetic  55.4 us (11%)
  blocking collectives  54.8 us (11%)
  matrix products  29.8 us (6%)
    ppermute x30, waiting for transfers between devices, hop(): lax.ppermute(array, 'fsdp', [(i, K * (i // K ^ d) + i % K) for i in range...  94.1 us
    ppermute x3, waiting for transfers between devices, ring_scatter(): arrived = lax.ppermute(total.astype(bf16), 'ctx', ring_pairs)  56.1 us
    psum x1, blocking collectives, local(): vector_total = lax.psum(vector_total, ('ctx', 'fsdp'))  54.8 us
    ppermute x30, starting transfers between devices, hop(): lax.ppermute(array, 'fsdp', [(i, K * (i // K ^ d) + i % K) for i in range...  40.3 us
    ppermute x4, waiting for transfers between devices, swap(): return lax.ppermute(array, ('ctx', 'fsdp'), swap_pairs)  34.5 us
    ppermute x3, waiting for transfers between devices, ring_gather(): held.append(lax.ppermute(held[-1], 'ctx', ring_pairs))  33.8 us
    ppermute x4, starting transfers between devices, swap(): return lax.ppermute(array, ('ctx', 'fsdp'), swap_pairs)  23.6 us
    sub x2, other arithmetic, adam_update(): weights - learn_rate * (first_hat / (jnp.sqrt(second_hat) + adam_eps) + d...  20.3 us
  transfers between devices with their start and end apart: 42, of which 26 were waited for; matrix products, arithmetic and copies ran while one was open for 6% of the time, Pallas kernels for 0%

profile of v1, /device:TPU:14, one launch (start us, length us, event | category | flops | bytes accessed | tf_op | source)
XLA Modules:
  0.0 499.8 jit_solution(3836520633291708315)
XLA Ops:
  4.0 3.9 reshape.276
  10.6 6.1 %copy.70 = bf16[3,4,128,4,2,128]{2,5,4,3,0,1:T(8,128)(2,1)} copy(bf16[3,4,128,4,2,128]{5,1,4,2,3,0:T(4,128)(2,1)} %bitcast.192) | data formatting | bytes 6291456 | tf_op jit(solution)/shard_map/transpose | solution.py:144
  22.8 17.8 %collective-permute-done.6 = bf16[3,128,1024]{1,2,0:T(8,128)(2,1)S(1)} collective-permute-done((bf16[3,128,1024]{1,2,0:T(8,128)(2,1)S(1)}, bf16[3,128,1024]{1,2,0:T(8,128)(2,1)S(1)}, u32[]{:S(2)}, u32[]{:S(2)}) %collective-permute-start.6) | collective-permute-done | bytes 786464 | tf_op jit(solution)/shard_map/ppermute | solution.py:107
  40.6 15.0 %collective-permute-done.5 = bf16[3,128,1024]{1,2,0:T(8,128)(2,1)S(1)} collective-permute-done((bf16[3,128,1024]{1,2,0:T(8,128)(2,1)S(1)}, bf16[3,128,1024]{1,2,0:T(8,128)(2,1)S(1)}, u32[]{:S(2)}, u32[]{:S(2)}) %collective-permute-start.5) | collective-permute-done | bytes 786464 | tf_op jit(solution)/shard_map/ppermute | solution.py:107
  57.6 5.2 %collective-permute-start = (bf16[128,1024]{1,0:T(8,128)(2,1)S(1)}, bf16[128,1024]{1,0:T(8,128)(2,1)S(1)}, u32[]{:S(2)}, u32[]{:S(2)}) collective-permute-start(bf16[128,1024]{1,0:T(8,128)(2,1)S(1)} %bitcast.265), channel_id=1, source_target_pairs={{0,0},{1,1},{2,8},{3,9},{4,16},{5,17},{6,24},{7,25},{8,2},{9,3},{1... | collective-permute-start | bytes 786440 | tf_op jit(solution)/shard_map/ppermute | solution.py:104
  62.8 11.9 %collective-permute-done = bf16[128,1024]{1,0:T(8,128)(2,1)S(1)} collective-permute-done((bf16[128,1024]{1,0:T(8,128)(2,1)S(1)}, bf16[128,1024]{1,0:T(8,128)(2,1)S(1)}, u32[]{:S(2)}, u32[]{:S(2)}) %collective-permute-start) | collective-permute-done | bytes 262176 | tf_op jit(solution)/shard_map/ppermute | solution.py:104
  84.5 7.8 %collective-permute-done.2 = bf16[128,1024]{1,0:T(8,128)(2,1)} collective-permute-done((bf16[128,1024]{1,0:T(8,128)(2,1)S(1)}, bf16[128,1024]{1,0:T(8,128)(2,1)}, u32[]{:S(2)}, u32[]{:S(2)}) %collective-permute-start.2) | collective-permute-done | bytes 262176 | tf_op jit(solution)/shard_map/ppermute | solution.py:107
  96.0 4.7 fusion.20
  137.4 4.9 collective-permute-done.13
  154.7 7.7 %collective-permute-start.18 = (bf16[128,1024]{1,0:T(8,128)(2,1)S(1)}, bf16[128,1024]{1,0:T(8,128)(2,1)S(1)}, u32[]{:S(2)}, u32[]{:S(2)}) collective-permute-start(bf16[128,1024]{1,0:T(8,128)(2,1)S(1)} %bitcast.266), channel_id=1, source_target_pairs={{0,0},{1,1},{2,8},{3,9},{4,16},{5,17},{6,24},{7,25},{8,2},{9,3},{1... | collective-permute-start | bytes 786440 | tf_op jit(solution)/shard_map/ppermute | solution.py:104
  162.5 8.8 %collective-permute-done.15 = bf16[128,1024]{1,0:T(8,128)(2,1)S(1)} collective-permute-done((bf16[128,1024]{1,0:T(8,128)(2,1)S(1)}, bf16[128,1024]{1,0:T(8,128)(2,1)S(1)}, u32[]{:S(2)}, u32[]{:S(2)}) %collective-permute-start.15) | collective-permute-done | bytes 262176 | tf_op jit(solution)/shard_map/ppermute | solution.py:107
  173.6 5.8 %collective-permute-start.21 = (bf16[128,1024]{1,0:T(8,128)(2,1)S(1)}, bf16[128,1024]{1,0:T(8,128)(2,1)S(1)}, u32[]{:S(2)}, u32[]{:S(2)}) collective-permute-start(bf16[128,1024]{1,0:T(8,128)(2,1)S(1)} %convert_element_type.188), channel_id=1, source_target_pairs={{0,6},{1,7},{2,4},{3,5},{4,2},{5,3},{6,0},{7,1},{8,14},{9,15},{10,... | collective-permute-start | bytes 786440 | tf_op jit(solution)/shard_map/ppermute | solution.py:107
  180.1 6.6 %collective-permute-done.21 = bf16[128,1024]{1,0:T(8,128)(2,1)S(1)} collective-permute-done((bf16[128,1024]{1,0:T(8,128)(2,1)S(1)}, bf16[128,1024]{1,0:T(8,128)(2,1)S(1)}, u32[]{:S(2)}, u32[]{:S(2)}) %collective-permute-start.21) | collective-permute-done | bytes 262176 | tf_op jit(solution)/shard_map/ppermute | solution.py:107
  190.5 5.2 %fusion.94 = (f32[1024]{0:T(1024)S(1)}, bf16[512,1024]{1,0:T(8,128)(2,1)S(1)}) fusion(f32[512,1024]{1,0:T(8,128)} %get-tuple-element.96, f32[1024]{0:T(1024)S(1)} %bitcast.264, bf16[1024,1024]{1,0:T(8,128)(2,1)} %bitcast.211, bf16[128,1024]{1,0:T(8,128)(2,1)S(1)} %collective-permute-done.21, bf16[128,1024]{1,0:T(8,128)(2,1)S(1)} %collective-permute-done.20, ...), kind=kOutput, calls=%fused_computation.204 | convolution fusion | flops 1084226560 | bytes 6299648 | tf_op jit(solution)/shard_map/dot_general | solution.py:25
  203.3 4.0 collective-permute-done.24
  207.3 4.4 collective-permute-done.23
  218.7 4.0 collective-permute-done.27
  222.7 4.4 collective-permute-done.26
  239.6 6.0 %collective-permute-done.32 = bf16[4,384,1024]{2,1,0:T(8,128)(2,1)} collective-permute-done((bf16[4,384,1024]{2,1,0:T(8,128)(2,1)}, bf16[4,384,1024]{2,1,0:T(8,128)(2,1)}, u32[]{:S(2)}, u32[]{:S(2)}) %collective-permute-start.32) | collective-permute-done | bytes 3145760 | tf_op jit(solution)/shard_map/ppermute | solution.py:121
  245.6 4.3 convert_add_fusion
  255.3 17.6 %collective-permute-done.33 = bf16[4,3,32,1024]{3,2,1,0:T(8,128)(2,1)S(1)} collective-permute-done((bf16[4,3,32,1024]{3,2,1,0:T(8,128)(2,1)S(1)}, bf16[4,3,32,1024]{3,2,1,0:T(8,128)(2,1)S(1)}, u32[]{:S(2)}, u32[]{:S(2)}) %collective-permute-start.33) | collective-permute-done | bytes 786464 | tf_op jit(solution)/shard_map/ppermute | solution.py:128
  276.6 18.7 %collective-permute-done.34 = bf16[4,3,32,1024]{3,2,1,0:T(8,128)(2,1)S(1)} collective-permute-done((bf16[4,3,32,1024]{3,2,1,0:T(8,128)(2,1)S(1)}, bf16[4,3,32,1024]{3,2,1,0:T(8,128)(2,1)S(1)}, u32[]{:S(2)}, u32[]{:S(2)}) %collective-permute-start.34) | collective-permute-done | bytes 786464 | tf_op jit(solution)/shard_map/ppermute | solution.py:128
  297.1 19.7 %collective-permute-done.35 = bf16[4,3,32,1024]{3,2,1,0:T(8,128)(2,1)S(1)} collective-permute-done((bf16[4,3,32,1024]{3,2,1,0:T(8,128)(2,1)S(1)}, bf16[4,3,32,1024]{3,2,1,0:T(8,128)(2,1)S(1)}, u32[]{:S(2)}, u32[]{:S(2)}) %collective-permute-start.35) | collective-permute-done | bytes 786464 | tf_op jit(solution)/shard_map/ppermute | solution.py:128
  322.1 4.4 collective-permute-done.38
  329.1 19.5 %collective-permute-done.39 = bf16[3,4,32,1024]{3,2,1,0:T(8,128)(2,1)S(1)} collective-permute-done((bf16[3,4,32,1024]{3,2,1,0:T(8,128)(2,1)S(1)}, bf16[3,4,32,1024]{3,2,1,0:T(8,128)(2,1)S(1)}, u32[]{:S(2)}, u32[]{:S(2)}) %collective-permute-start.39) | collective-permute-done | bytes 786464 | tf_op jit(solution)/shard_map/ppermute | solution.py:135
  353.3 14.3 %collective-permute-done.40 = bf16[3,4,32,1024]{3,2,1,0:T(8,128)(2,1)S(1)} collective-permute-done((bf16[3,4,32,1024]{3,2,1,0:T(8,128)(2,1)S(1)}, bf16[3,4,32,1024]{3,2,1,0:T(8,128)(2,1)S(1)}, u32[]{:S(2)}, u32[]{:S(2)}) %collective-permute-start.40) | collective-permute-done | bytes 786464 | tf_op jit(solution)/shard_map/ppermute | solution.py:135
  367.5 8.8 %collective-permute-start.17 = (bf16[128,1024]{1,0:T(8,128)(2,1)S(1)}, bf16[128,1024]{1,0:T(8,128)(2,1)}, u32[]{:S(2)}, u32[]{:S(2)}) collective-permute-start(bf16[128,1024]{1,0:T(8,128)(2,1)S(1)} %copy-done.26), channel_id=1, source_target_pairs={{0,0},{1,1},{2,8},{3,9},{4,16},{5,17},{6,24},{7,25},{8,2},{9,3},{1... | collective-permute-start | bytes 786440 | tf_op jit(solution)/shard_map/ppermute | solution.py:104
  379.3 22.2 %collective-permute-done.17 = bf16[128,1024]{1,0:T(8,128)(2,1)} collective-permute-done((bf16[128,1024]{1,0:T(8,128)(2,1)S(1)}, bf16[128,1024]{1,0:T(8,128)(2,1)}, u32[]{:S(2)}, u32[]{:S(2)}) %collective-permute-start.17) | collective-permute-done | bytes 262176 | tf_op jit(solution)/shard_map/ppermute | solution.py:104
  401.9 54.8 %psum.7 = f32[12,1024]{1,0:T(8,128)S(1)} all-reduce(f32[12,1024]{1,0:T(8,128)S(1)} %concatenate.41), channel_id=1, replica_groups=mesh['ctx'=4,'fsdp'=8] {'ctx','fsdp'}, use_global_device_ids=true, to_apply=%region_20.21 | all-reduce | flops 12288 | bytes 98304 | tf_op jit(solution)/shard_map/psum | solution.py:282
  465.5 7.6 %copy.111 = bf16[3,4,128,4,2,128]{5,1,4,2,3,0:T(4,128)(2,1)} copy(bf16[3,4,128,4,2,128]{5,4,3,2,1,0:T(2,128)(2,1)} %reshape_reshape.13) | data formatting | bytes 6291456 | tf_op jit(solution)/shard_map/reshape;reshape | solution.py:148
  473.1 6.1 %reshape.303 = bf16[1536,1024]{1,0:T(8,128)(2,1)} reshape(bf16[3,4,128,2,4,128]{5,4,3,2,1,0:T(4,128)(2,1)} %bitcast.193) | data formatting | bytes 6291456 | tf_op jit(solution)/shard_map/reshape | solution.py:148
  479.2 18.7 %multiply_subtract_fusion = (f32[1536,1024]{1,0:T(8,128)}, f32[1536,1024]{1,0:T(8,128)}, f32[1536,1024]{1,0:T(8,128)}, f32[1536,1024]{1,0:T(8,128)}) fusion(f32[1536,1024]{1,0:T(8,128)} %param.10, f32[1536,1024]{1,0:T(8,128)} %param.11, f32[1536,1024]{1,0:T(8,128)} %param.12, bf16[1536,1024]{1,0:T(8,128)(2,1)} %reshape.303, ...), kind=kLoop, calls=%fused_computation.20 | loop fusion | flops 26738688 | bytes 50333184 | tf_op jit(solution)/shard_map/sub | solution.py:55
  (292 shorter events, 146.7 us)
Async XLA Ops:
  19.2 21.4 %collective-permute-start.6 = (bf16[3,128,1024]{1,2,0:T(8,128)(2,1)S(1)}, bf16[3,128,1024]{1,2,0:T(8,128)(2,1)S(1)}, u32[]{:S(2)}, u32[]{:S(2)}) collective-permute-start(bf16[3,128,1024]{1,2,0:T(8,128)(2,1)S(1)} %get-tuple-element.49), channel_id=1, source_target_pairs={{0,6},{1,7},{2,4},{3,5},{4,2},{5,3},{6,0},{7,1},{8,14},{9,15},{10,... | collective-permute-start | bytes 2359304 | tf_op jit(solution)/shard_map/ppermute | solution.py:107
  19.8 35.9 %collective-permute-start.5 = (bf16[3,128,1024]{1,2,0:T(8,128)(2,1)S(1)}, bf16[3,128,1024]{1,2,0:T(8,128)(2,1)S(1)}, u32[]{:S(2)}, u32[]{:S(2)}) collective-permute-start(bf16[3,128,1024]{1,2,0:T(8,128)(2,1)S(1)} %get-tuple-element.50), channel_id=1, source_target_pairs={{0,4},{1,5},{2,6},{3,7},{4,0},{5,1},{6,2},{7,3},{8,12},{9,13},{10,... | collective-permute-start | bytes 2359304 | tf_op jit(solution)/shard_map/ppermute | solution.py:107
  21.3 34.3 %collective-permute-start.4 = (bf16[3,128,1024]{1,2,0:T(8,128)(2,1)S(1)}, bf16[3,128,1024]{1,2,0:T(8,128)(2,1)S(1)}, u32[]{:S(2)}, u32[]{:S(2)}) collective-permute-start(bf16[3,128,1024]{1,2,0:T(8,128)(2,1)S(1)} %get-tuple-element.51), channel_id=1, source_target_pairs={{0,2},{1,3},{2,0},{3,1},{4,6},{5,7},{6,4},{7,5},{8,10},{9,11},{10,... | collective-permute-start | bytes 2359304 | tf_op jit(solution)/shard_map/ppermute | solution.py:107
  57.5 36.8 %collective-permute-start.7 = (bf16[4,3,128,1024]{2,3,1,0:T(8,128)(2,1)}, bf16[4,3,128,1024]{2,3,1,0:T(8,128)(2,1)}, u32[]{:S(2)}, u32[]{:S(2)}) collective-permute-start(bf16[4,3,128,1024]{2,3,1,0:T(8,128)(2,1)} %get-tuple-element.46), channel_id=1, source_target_pairs={{0,1},{1,0},{2,3},{3,2},{4,5},{5,4},{6,7},{7,6},{8,9},{9,8},{10,11... | collective-permute-start | bytes 9437192 | tf_op jit(solution)/shard_map/ppermute | solution.py:121
  57.6 17.1 %collective-permute-start = (bf16[128,1024]{1,0:T(8,128)(2,1)S(1)}, bf16[128,1024]{1,0:T(8,128)(2,1)S(1)}, u32[]{:S(2)}, u32[]{:S(2)}) collective-permute-start(bf16[128,1024]{1,0:T(8,128)(2,1)S(1)} %bitcast.265), channel_id=1, source_target_pairs={{0,0},{1,1},{2,8},{3,9},{4,16},{5,17},{6,24},{7,25},{8,2},{9,3},{1... | collective-permute-start | bytes 786440 | tf_op jit(solution)/shard_map/ppermute | solution.py:104
  77.4 14.9 %collective-permute-start.2 = (bf16[128,1024]{1,0:T(8,128)(2,1)S(1)}, bf16[128,1024]{1,0:T(8,128)(2,1)}, u32[]{:S(2)}, u32[]{:S(2)}) collective-permute-start(bf16[128,1024]{1,0:T(8,128)(2,1)S(1)} %collective-permute-done), channel_id=1, source_target_pairs={{0,4},{1,5},{2,6},{3,7},{4,0},{5,1},{6,2},{7,3},{8,12},{9,13},{10,... | collective-permute-start | bytes 786440 | tf_op jit(solution)/shard_map/ppermute | solution.py:107
  81.3 12.0 %collective-permute-start.3 = (bf16[128,1024]{1,0:T(8,128)(2,1)S(1)}, bf16[128,1024]{1,0:T(8,128)(2,1)S(1)}, u32[]{:S(2)}, u32[]{:S(2)}) collective-permute-start(bf16[128,1024]{1,0:T(8,128)(2,1)S(1)} %collective-permute-done), channel_id=1, source_target_pairs={{0,6},{1,7},{2,4},{3,5},{4,2},{5,3},{6,0},{7,1},{8,14},{9,15},{10,... | collective-permute-start | bytes 786440 | tf_op jit(solution)/shard_map/ppermute | solution.py:107
  113.6 16.5 %collective-permute-start.10 = (bf16[128,1024]{1,0:T(8,128)(2,1)}, bf16[128,1024]{1,0:T(8,128)(2,1)}, u32[]{:S(2)}, u32[]{:S(2)}) collective-permute-start(bf16[128,1024]{1,0:T(8,128)(2,1)} %get-tuple-element.64), channel_id=1, source_target_pairs={{0,6},{1,7},{2,4},{3,5},{4,2},{5,3},{6,0},{7,1},{8,14},{9,15},{10,... | collective-permute-start | bytes 786440 | tf_op jit(solution)/shard_map/ppermute | solution.py:107
  115.1 15.0 %collective-permute-start.9 = (bf16[128,1024]{1,0:T(8,128)(2,1)}, bf16[128,1024]{1,0:T(8,128)(2,1)}, u32[]{:S(2)}, u32[]{:S(2)}) collective-permute-start(bf16[128,1024]{1,0:T(8,128)(2,1)} %get-tuple-element.65), channel_id=1, source_target_pairs={{0,4},{1,5},{2,6},{3,7},{4,0},{5,1},{6,2},{7,3},{8,12},{9,13},{10,... | collective-permute-start | bytes 786440 | tf_op jit(solution)/shard_map/ppermute | solution.py:107
  115.4 14.8 %collective-permute-start.8 = (bf16[128,1024]{1,0:T(8,128)(2,1)}, bf16[128,1024]{1,0:T(8,128)(2,1)}, u32[]{:S(2)}, u32[]{:S(2)}) collective-permute-start(bf16[128,1024]{1,0:T(8,128)(2,1)} %get-tuple-element.63), channel_id=1, source_target_pairs={{0,2},{1,3},{2,0},{3,1},{4,6},{5,7},{6,4},{7,5},{8,10},{9,11},{10,... | collective-permute-start | bytes 786440 | tf_op jit(solution)/shard_map/ppermute | solution.py:107
  133.7 12.1 %collective-permute-start.12 = (bf16[128,1024]{1,0:T(8,128)(2,1)S(1)}, bf16[128,1024]{1,0:T(8,128)(2,1)S(1)}, u32[]{:S(2)}, u32[]{:S(2)}) collective-permute-start(bf16[128,1024]{1,0:T(8,128)(2,1)S(1)} %fusion.52), channel_id=1, source_target_pairs={{0,4},{1,5},{2,6},{3,7},{4,0},{5,1},{6,2},{7,3},{8,12},{9,13},{10,... | collective-permute-start | bytes 786440 | tf_op jit(solution)/shard_map/ppermute | solution.py:107
  134.0 12.1 %collective-permute-start.11 = (bf16[128,1024]{1,0:T(8,128)(2,1)S(1)}, bf16[128,1024]{1,0:T(8,128)(2,1)S(1)}, u32[]{:S(2)}, u32[]{:S(2)}) collective-permute-start(bf16[128,1024]{1,0:T(8,128)(2,1)S(1)} %fusion.52), channel_id=1, source_target_pairs={{0,2},{1,3},{2,0},{3,1},{4,6},{5,7},{6,4},{7,5},{8,10},{9,11},{10,... | collective-permute-start | bytes 786440 | tf_op jit(solution)/shard_map/ppermute | solution.py:107
  151.2 11.3 %collective-permute-start.16 = (bf16[128,1024]{1,0:T(8,128)(2,1)S(1)}, bf16[128,1024]{1,0:T(8,128)(2,1)S(1)}, u32[]{:S(2)}, u32[]{:S(2)}) collective-permute-start(bf16[128,1024]{1,0:T(8,128)(2,1)S(1)} %get-tuple-element.61), channel_id=1, source_target_pairs={{0,6},{1,7},{2,4},{3,5},{4,2},{5,3},{6,0},{7,1},{8,14},{9,15},{10,... | collective-permute-start | bytes 786440 | tf_op jit(solution)/shard_map/ppermute | solution.py:107
  152.7 18.6 %collective-permute-start.15 = (bf16[128,1024]{1,0:T(8,128)(2,1)S(1)}, bf16[128,1024]{1,0:T(8,128)(2,1)S(1)}, u32[]{:S(2)}, u32[]{:S(2)}) collective-permute-start(bf16[128,1024]{1,0:T(8,128)(2,1)S(1)} %get-tuple-element.62), channel_id=1, source_target_pairs={{0,4},{1,5},{2,6},{3,7},{4,0},{5,1},{6,2},{7,3},{8,12},{9,13},{10,... | collective-permute-start | bytes 786440 | tf_op jit(solution)/shard_map/ppermute | solution.py:107
  153.3 18.0 %collective-permute-start.14 = (bf16[128,1024]{1,0:T(8,128)(2,1)S(1)}, bf16[128,1024]{1,0:T(8,128)(2,1)S(1)}, u32[]{:S(2)}, u32[]{:S(2)}) collective-permute-start(bf16[128,1024]{1,0:T(8,128)(2,1)S(1)} %get-tuple-element.60), channel_id=1, source_target_pairs={{0,2},{1,3},{2,0},{3,1},{4,6},{5,7},{6,4},{7,5},{8,10},{9,11},{10,... | collective-permute-start | bytes 786440 | tf_op jit(solution)/shard_map/ppermute | solution.py:107
  154.7 17.6 %collective-permute-start.18 = (bf16[128,1024]{1,0:T(8,128)(2,1)S(1)}, bf16[128,1024]{1,0:T(8,128)(2,1)S(1)}, u32[]{:S(2)}, u32[]{:S(2)}) collective-permute-start(bf16[128,1024]{1,0:T(8,128)(2,1)S(1)} %bitcast.266), channel_id=1, source_target_pairs={{0,0},{1,1},{2,8},{3,9},{4,16},{5,17},{6,24},{7,25},{8,2},{9,3},{1... | collective-permute-start | bytes 786440 | tf_op jit(solution)/shard_map/ppermute | solution.py:104
  173.6 13.1 %collective-permute-start.21 = (bf16[128,1024]{1,0:T(8,128)(2,1)S(1)}, bf16[128,1024]{1,0:T(8,128)(2,1)S(1)}, u32[]{:S(2)}, u32[]{:S(2)}) collective-permute-start(bf16[128,1024]{1,0:T(8,128)(2,1)S(1)} %convert_element_type.188), channel_id=1, source_target_pairs={{0,6},{1,7},{2,4},{3,5},{4,2},{5,3},{6,0},{7,1},{8,14},{9,15},{10,... | collective-permute-start | bytes 786440 | tf_op jit(solution)/shard_map/ppermute | solution.py:107
  199.0 12.7 %collective-permute-start.23 = (bf16[128,1024]{1,0:T(8,128)(2,1)S(1)}, bf16[128,1024]{1,0:T(8,128)(2,1)S(1)}, u32[]{:S(2)}, u32[]{:S(2)}) collective-permute-start(bf16[128,1024]{1,0:T(8,128)(2,1)S(1)} %get-tuple-element.59), channel_id=1, source_target_pairs={{0,4},{1,5},{2,6},{3,7},{4,0},{5,1},{6,2},{7,3},{8,12},{9,13},{10,... | collective-permute-start | bytes 786440 | tf_op jit(solution)/shard_map/ppermute | solution.py:107
  200.4 11.4 %collective-permute-start.22 = (bf16[128,1024]{1,0:T(8,128)(2,1)S(1)}, bf16[128,1024]{1,0:T(8,128)(2,1)S(1)}, u32[]{:S(2)}, u32[]{:S(2)}) collective-permute-start(bf16[128,1024]{1,0:T(8,128)(2,1)S(1)} %get-tuple-element.57), channel_id=1, source_target_pairs={{0,2},{1,3},{2,0},{3,1},{4,6},{5,7},{6,4},{7,5},{8,10},{9,11},{10,... | collective-permute-start | bytes 786440 | tf_op jit(solution)/shard_map/ppermute | solution.py:107
  213.7 13.4 %collective-permute-start.26 = (bf16[128,1024]{1,0:T(8,128)(2,1)S(1)}, bf16[128,1024]{1,0:T(8,128)(2,1)S(1)}, u32[]{:S(2)}, u32[]{:S(2)}) collective-permute-start(bf16[128,1024]{1,0:T(8,128)(2,1)S(1)} %convert_element_type.194), channel_id=1, source_target_pairs={{0,4},{1,5},{2,6},{3,7},{4,0},{5,1},{6,2},{7,3},{8,12},{9,13},{10,... | collective-permute-start | bytes 786440 | tf_op jit(solution)/shard_map/ppermute | solution.py:107
  214.3 12.8 %collective-permute-start.25 = (bf16[128,1024]{1,0:T(8,128)(2,1)S(1)}, bf16[128,1024]{1,0:T(8,128)(2,1)S(1)}, u32[]{:S(2)}, u32[]{:S(2)}) collective-permute-start(bf16[128,1024]{1,0:T(8,128)(2,1)S(1)} %convert_element_type.194), channel_id=1, source_target_pairs={{0,2},{1,3},{2,0},{3,1},{4,6},{5,7},{6,4},{7,5},{8,10},{9,11},{10,... | collective-permute-start | bytes 786440 | tf_op jit(solution)/shard_map/ppermute | solution.py:107
  252.7 20.2 %collective-permute-start.33 = (bf16[4,3,32,1024]{3,2,1,0:T(8,128)(2,1)S(1)}, bf16[4,3,32,1024]{3,2,1,0:T(8,128)(2,1)S(1)}, u32[]{:S(2)}, u32[]{:S(2)}) collective-permute-start(bf16[4,3,32,1024]{3,2,1,0:T(8,128)(2,1)S(1)} %fusion.21), channel_id=1, source_target_pairs={{0,8},{8,16},{16,24},{24,0},{1,9},{9,17},{17,25},{25,1},{2,10},{10... | collective-permute-start | bytes 2359304 | tf_op jit(solution)/shard_map/ppermute | solution.py:128
  274.6 20.8 %collective-permute-start.34 = (bf16[4,3,32,1024]{3,2,1,0:T(8,128)(2,1)S(1)}, bf16[4,3,32,1024]{3,2,1,0:T(8,128)(2,1)S(1)}, u32[]{:S(2)}, u32[]{:S(2)}) collective-permute-start(bf16[4,3,32,1024]{3,2,1,0:T(8,128)(2,1)S(1)} %fusion.10), channel_id=1, source_target_pairs={{0,8},{8,16},{16,24},{24,0},{1,9},{9,17},{17,25},{25,1},{2,10},{10... | collective-permute-start | bytes 2359304 | tf_op jit(solution)/shard_map/ppermute | solution.py:128
  297.0 19.8 %collective-permute-start.35 = (bf16[4,3,32,1024]{3,2,1,0:T(8,128)(2,1)S(1)}, bf16[4,3,32,1024]{3,2,1,0:T(8,128)(2,1)S(1)}, u32[]{:S(2)}, u32[]{:S(2)}) collective-permute-start(bf16[4,3,32,1024]{3,2,1,0:T(8,128)(2,1)S(1)} %fusion.9), channel_id=1, source_target_pairs={{0,8},{8,16},{16,24},{24,0},{1,9},{9,17},{17,25},{25,1},{2,10},{10... | collective-permute-start | bytes 2359304 | tf_op jit(solution)/shard_map/ppermute | solution.py:128
  329.0 19.6 %collective-permute-start.39 = (bf16[3,4,32,1024]{3,2,1,0:T(8,128)(2,1)S(1)}, bf16[3,4,32,1024]{3,2,1,0:T(8,128)(2,1)S(1)}, u32[]{:S(2)}, u32[]{:S(2)}) collective-permute-start(bf16[3,4,32,1024]{3,2,1,0:T(8,128)(2,1)S(1)} %get-tuple-element.67), channel_id=1, source_target_pairs={{0,8},{8,16},{16,24},{24,0},{1,9},{9,17},{17,25},{25,1},{2,10},{10... | collective-permute-start | bytes 2359304 | tf_op jit(solution)/shard_map/ppermute | solution.py:135
  348.6 18.9 %collective-permute-start.40 = (bf16[3,4,32,1024]{3,2,1,0:T(8,128)(2,1)S(1)}, bf16[3,4,32,1024]{3,2,1,0:T(8,128)(2,1)S(1)}, u32[]{:S(2)}, u32[]{:S(2)}) collective-permute-start(bf16[3,4,32,1024]{3,2,1,0:T(8,128)(2,1)S(1)} %collective-permute-done.39), channel_id=1, source_target_pairs={{0,8},{8,16},{16,24},{24,0},{1,9},{9,17},{17,25},{25,1},{2,10},{10... | collective-permute-start | bytes 2359304 | tf_op jit(solution)/shard_map/ppermute | solution.py:135
  349.7 26.6 %collective-permute-start.30 = (bf16[128,1024]{1,0:T(8,128)(2,1)S(1)}, bf16[128,1024]{1,0:T(8,128)(2,1)S(1)}, u32[]{:S(2)}, u32[]{:S(2)}) collective-permute-start(bf16[128,1024]{1,0:T(8,128)(2,1)S(1)} %get-tuple-element.55), channel_id=1, source_target_pairs={{0,6},{1,7},{2,4},{3,5},{4,2},{5,3},{6,0},{7,1},{8,14},{9,15},{10,... | collective-permute-start | bytes 786440 | tf_op jit(solution)/shard_map/ppermute | solution.py:107
  350.7 25.7 %collective-permute-start.29 = (bf16[128,1024]{1,0:T(8,128)(2,1)S(1)}, bf16[128,1024]{1,0:T(8,128)(2,1)S(1)}, u32[]{:S(2)}, u32[]{:S(2)}) collective-permute-start(bf16[128,1024]{1,0:T(8,128)(2,1)S(1)} %get-tuple-element.56), channel_id=1, source_target_pairs={{0,4},{1,5},{2,6},{3,7},{4,0},{5,1},{6,2},{7,3},{8,12},{9,13},{10,... | collective-permute-start | bytes 786440 | tf_op jit(solution)/shard_map/ppermute | solution.py:107
  352.1 24.3 %collective-permute-start.28 = (bf16[128,1024]{1,0:T(8,128)(2,1)S(1)}, bf16[128,1024]{1,0:T(8,128)(2,1)S(1)}, u32[]{:S(2)}, u32[]{:S(2)}) collective-permute-start(bf16[128,1024]{1,0:T(8,128)(2,1)S(1)} %get-tuple-element.54), channel_id=1, source_target_pairs={{0,2},{1,3},{2,0},{3,1},{4,6},{5,7},{6,4},{7,5},{8,10},{9,11},{10,... | collective-permute-start | bytes 786440 | tf_op jit(solution)/shard_map/ppermute | solution.py:107
  367.5 91.7 %collective-permute-start.41 = (bf16[3,4,32,1024]{3,2,1,0:T(8,128)(2,1)S(1)}, bf16[3,4,32,1024]{3,2,1,0:T(8,128)(2,1)}, u32[]{:S(2)}, u32[]{:S(2)}) collective-permute-start(bf16[3,4,32,1024]{3,2,1,0:T(8,128)(2,1)S(1)} %collective-permute-done.40), channel_id=1, source_target_pairs={{0,8},{8,16},{16,24},{24,0},{1,9},{9,17},{17,25},{25,1},{2,10},{10... | collective-permute-start | bytes 2359304 | tf_op jit(solution)/shard_map/ppermute | solution.py:135
  367.5 34.0 %collective-permute-start.17 = (bf16[128,1024]{1,0:T(8,128)(2,1)S(1)}, bf16[128,1024]{1,0:T(8,128)(2,1)}, u32[]{:S(2)}, u32[]{:S(2)}) collective-permute-start(bf16[128,1024]{1,0:T(8,128)(2,1)S(1)} %copy-done.26), channel_id=1, source_target_pairs={{0,0},{1,1},{2,8},{3,9},{4,16},{5,17},{6,24},{7,25},{8,2},{9,3},{1... | collective-permute-start | bytes 786440 | tf_op jit(solution)/shard_map/ppermute | solution.py:104
  377.3 81.1 %collective-permute-start.31 = (bf16[128,1024]{1,0:T(8,128)(2,1)}, bf16[128,1024]{1,0:T(8,128)(2,1)S(1)}, u32[]{:S(2)}, u32[]{:S(2)}) collective-permute-start(bf16[128,1024]{1,0:T(8,128)(2,1)} %fusion.35), channel_id=1, source_target_pairs={{0,0},{1,1},{2,8},{3,9},{4,16},{5,17},{6,24},{7,25},{8,2},{9,3},{1... | collective-permute-start | bytes 786440 | tf_op jit(solution)/shard_map/ppermute | solution.py:104
  (71 other events, 545.6 us)

commit v2 on v1

--- a/solution.py
+++ b/solution.py
@@ -3,6 +3,8 @@
 import jax
 import jax.numpy as jnp
 from jax import lax
+from jax.experimental import pallas as pl
+from jax.experimental.pallas import tpu as pltpu
 from jax.sharding import PartitionSpec as P
 
 D = 1024
@@ -60,6 +62,131 @@
 
 def at(array, index, axis=0):
     return lax.dynamic_index_in_dim(array, index, axis, keepdims=False)
+
+
+def pack_kernel(C, s, per, nb, bounds, place, rows_ref, out_ref):
+    slot = pl.program_id(1)
+    owner = slot ^ place[0]
+    block = nb * place[3] + pl.program_id(0)
+    by_column = (block >= bounds[0]) & (block < bounds[1])
+
+    @pl.when(jnp.logical_not(by_column))
+    def _():
+        start = pl.multiple_of(owner * s, s)
+        out_ref[0, 0] = rows_ref[pl.ds(start, s), :].astype(bf16)
+
+    @pl.when(by_column)
+    def _():
+        for m in range(C):
+            for h in range(per):
+                start = pl.multiple_of((h * C + owner) * s, s)
+                to = (m * per + h) * s
+                out_ref[0, 0, :, to : to + s] = rows_ref[
+                    m * s : (m + 1) * s, pl.ds(start, s)
+                ].astype(bf16)
+
+
+def pack(place, rows, C, s, per, nb, bounds):
+    width = rows.shape[1]
+    return pl.pallas_call(
+        lambda *refs: pack_kernel(C, s, per, nb, bounds, *refs),
+        out_shape=jax.ShapeDtypeStruct((C, nb, s, width), bf16),
+        grid_spec=pltpu.PrefetchScalarGridSpec(
+            num_scalar_prefetch=1,
+            grid=(nb, C),
+            in_specs=[pl.BlockSpec((C * s, width), lambda b, d, place: (b, 0))],
+            out_specs=pl.BlockSpec((1, 1, s, width), lambda b, d, place: (d, b, 0, 0)),
+        ),
+        name="pack",
+    )(place, rows)
+
+
+def unpack_kernel(K, nb, place, *refs):
+    owner = pl.program_id(0) // nb
+    core = owner % K
+    out_ref = refs[-1]
+    for k in range(K):
+
+        @pl.when((place[1] + K - k) % K == core)
+        def _(k=k):
+            out_ref[...] = refs[k][0]
+
+
+def unpack(place, pieces, C, K, s, nb):
+    width = pieces[0].shape[-1]
+    spec = pl.BlockSpec(
+        (1, 1, s, width), lambda n, place: ((n // nb // K) ^ place[0], n % nb, 0, 0)
+    )
+    return pl.pallas_call(
+        lambda *refs: unpack_kernel(K, nb, *refs),
+        out_shape=jax.ShapeDtypeStruct((C * K * nb, s, width), bf16),
+        grid_spec=pltpu.PrefetchScalarGridSpec(
+            num_scalar_prefetch=1,
+            grid=(C * K * nb,),
+            in_specs=[spec] * K,
+            out_specs=pl.BlockSpec((1, s, width), lambda n, place: (n, 0, 0)),
+        ),
+        name="unpack",
+    )(place, *pieces)
+
+
+def update_kernel(C, K, s, per, nb, bounds, place, *refs):
+    by_row, by_col = refs[:K], refs[K : 2 * K]
+    weights_ref, first_ref, second_ref = refs[2 * K : 2 * K + 3]
+    grad_ref, weights_out, first_out, second_out = refs[2 * K + 3 :]
+    g, c, z, f = place[0], place[1], place[2], place[3]
+    block = nb * f + pl.program_id(0)
+    by_column = (block >= bounds[0]) & (block < bounds[1])
+    piece = s // K // C
+
+    def start_of(k, e):
+        return pl.multiple_of(((c + K - k) % K) * (s // K) + (z ^ e) * piece, piece)
+
+    @pl.when(jnp.logical_not(by_column))
+    def _():
+        for k in range(K):
+            for e in range(C):
+                grad_ref[pl.ds(start_of(k, e), piece), :] = by_row[k][0, 0, e].astype(f32)
+
+    @pl.when(by_column)
+    def _():
+        for k in range(K):
+            for e in range(C):
+                for d in range(C):
+                    for h in range(per):
+                        column = pl.multiple_of((h * C + (g ^ d)) * s, s)
+                        grad_ref[pl.ds(start_of(k, e), piece), pl.ds(column, s)] = by_col[k][
+                            d, 0, e, :, h * s : (h + 1) * s
+                        ].astype(f32)
+
+    new_weights, new_first, new_second = adam_update(
+        weights_ref[...], grad_ref[...], first_ref[...], second_ref[...]
+    )
+    weights_out[...] = new_weights
+    first_out[...] = new_first
+    second_out[...] = new_second
+
+
+def update(place, pieces, weights, first, second, C, K, s, per, nb, bounds):
+    rows, width = weights.shape
+    piece = s // K // C
+    row_spec = pl.BlockSpec(
+        (1, 1, C, piece, width), lambda b, m, place: (m ^ place[0], b, 0, 0, 0)
+    )
+    col_spec = pl.BlockSpec((C, 1, C, piece, per * s), lambda b, m, place: (0, b, 0, 0, m))
+    tile = pl.BlockSpec((s, width), lambda b, m, place: (b * C + m, 0))
+    whole = jax.ShapeDtypeStruct((rows, width), f32)
+    return pl.pallas_call(
+        lambda *refs: update_kernel(C, K, s, per, nb, bounds, *refs),
+        out_shape=[whole] * 4,
+        grid_spec=pltpu.PrefetchScalarGridSpec(
+            num_scalar_prefetch=1,
+            grid=(nb, C),
+            in_specs=[row_spec] * K + [col_spec] * K + [tile] * 3,
+            out_specs=[tile] * 4,
+        ),
+        name="update",
+    )(place, *pieces, *pieces, weights, first, second)
 
 
 def local(
@@ -93,15 +220,19 @@
     blocks = total_rows // B
     first_o, last_o = 3 * per, 4 * per
 
-    swap_pairs = [
-        (zz * F + K * gg + cc, gg * F + K * zz + cc)
+    there = [
+        (zz * F + K * gg + cc, gg * F + K * (zz ^ gg) + cc)
         for zz in range(C)
         for gg in range(C)
         for cc in range(K)
     ]
+    back = [(to, source) for source, to in there]
 
     def swap(array):
-        return lax.ppermute(array, ("ctx", "fsdp"), swap_pairs)
+        return lax.ppermute(array, ("ctx", "fsdp"), there)
+
+    def swap_back(array):
+        return lax.ppermute(array, ("ctx", "fsdp"), back)
 
     def hop(array, d):
         return lax.ppermute(array, "fsdp", [(i, K * ((i // K) ^ d) + i % K) for i in range(F)])
@@ -120,21 +251,31 @@
     def cores(array, k):
         return lax.ppermute(array, "fsdp", [(i, K * (i // K) + (i + k) % K) for i in range(F)])
 
-    ring_pairs = [(i, (i + 1) % C) for i in range(C)]
-
-    def ring_scatter(parts):
-        total = at(parts, (z + C - 1) % C)
-        for step in range(C - 1):
-            arrived = lax.ppermute(total.astype(bf16), "ctx", ring_pairs)
-            total = arrived.astype(f32) + at(parts, (z + 2 * C - 2 - step) % C)
-        return total
-
-    def ring_gather(block):
-        held = [block]
-        for _ in range(C - 1):
-            held.append(lax.ppermute(held[-1], "ctx", ring_pairs))
-        held = jnp.stack(held)
-        return [at(held, (z + C - zz) % C) for zz in range(C)]
+    def along(array, e):
+        return lax.ppermute(array, "ctx", [(i, i ^ e) for i in range(C)])
+
+    def all_sum(values):
+        for axis, size in (("fsdp", F), ("ctx", C)):
+            step = 1
+            while step < size:
+                values = values + lax.ppermute(
+                    values, axis, [(i, i ^ step) for i in range(size)]
+                )
+                step *= 2
+        return values
+
+    def reduce_blocks(slices_):
+        n = slices_.shape[0]
+        parts = slices_.reshape(n, K, s // K, D)
+        total = at(parts, c, 1)
+        for k in range(1, K):
+            total = total + cores(at(parts, (c + k) % K, 1).astype(bf16), k).astype(f32)
+        total = total.reshape(n, C, s // K // C, D)
+        summed = at(total, z, 1)
+        for e in range(1, C):
+            summed = summed + along(at(total, z ^ e, 1).astype(bf16), e).astype(f32)
+        summed = summed.astype(bf16)
+        return jnp.stack([summed] + [along(summed, e) for e in range(1, C)], axis=1)
 
     def row_form(rows):
         return rows.reshape(-1, C, s, D)
@@ -147,22 +288,18 @@
         n = blocks_.shape[0]
         return blocks_.reshape(n, C, s, C, per, s).transpose(0, 3, 2, 4, 1, 5).reshape(n, B, D)
 
-    block_ids = nb * f + jnp.arange(max(nb, 1))
-    is_o = ((block_ids >= first_o) & (block_ids < last_o))[:, None, None, None]
-
-    weights_b = weight_rows.astype(bf16)
+    bounds = (first_o, last_o)
+    place = jnp.stack([g, c, z, f]).astype(jnp.int32)
+
     if direct:
-        payload = jnp.where(is_o, column_form(weights_b), row_form(weights_b))
-        parts = [at(payload, g, 1)]
-        for d in range(1, C):
-            parts.append(hop(at(payload, g ^ d, 1), d))
-        mine = jnp.stack(parts)
-        both = jnp.stack([mine] + [cores(mine, k) for k in range(1, K)])
-        slices = jnp.concatenate(
-            [at(at(both, (c - cc) % K), gg ^ g) for gg in range(C) for cc in range(K)], axis=0
-        )
+        payload = pack(place, weight_rows, C, s, per, nb, bounds)
+        parts = [payload[0]] + [hop(payload[d], d) for d in range(1, C)]
+        pieces = [jnp.stack(parts)]
+        for k in range(1, K):
+            pieces.append(jnp.stack([cores(piece, k) for piece in parts]))
+        slices = unpack(place, pieces, C, K, s, nb)
     else:
-        full = lax.all_gather(weights_b, "fsdp", axis=0, tiled=True)
+        full = lax.all_gather(weight_rows.astype(bf16), "fsdp", axis=0, tiled=True)
         rows_part = at(row_form(full), g, 1)
         cols_part = at(column_form(full), g, 1)
         slices = jnp.concatenate(
@@ -232,7 +369,7 @@
     activ_b = (pre_act * cdf).astype(bf16)
     second_sum = hidden_in + scatter(mat_nn(activ_b, w_2)) + down_b
     normed_two, inverse_two = normalize(second_sum)
-    output = swap((normed_two * gain_two + shift_two).astype(bf16))
+    output = swap_back((normed_two * gain_two + shift_two).astype(bf16))
 
     grad_gain_two = jnp.sum(cotan * normed_two, axis=0)
     grad_shift_two = jnp.sum(cotan, axis=0)
@@ -262,7 +399,7 @@
     grad_value = join_heads(batched("hqk,hqd->hkd", probs_b, grad_att))
     grad_proj = jnp.concatenate([grad_query, grad_key, grad_value], axis=1).astype(bf16)
     grad_qkv_w = mat_tn(grad_proj, sequence)
-    grad_inputs = swap((grad_first + scatter(mat_nn(grad_proj, w_qkv))).astype(bf16))
+    grad_inputs = swap_back((grad_first + scatter(mat_nn(grad_proj, w_qkv))).astype(bf16))
 
     small = jnp.stack(
         [
@@ -279,43 +416,33 @@
     vector_total = jnp.concatenate(
         [small, place_features(grad_up_b, hidden).reshape(-1, D)], axis=0
     )
-    vector_total = lax.psum(vector_total, ("ctx", "fsdp"))
+    vector_total = all_sum(vector_total)
     new_vectors, new_vfirst, new_vsecond = adam_update(
         vector_rows, vector_total, vector_first, vector_second
     )
 
-    grad_blocks = jnp.concatenate(
-        [
-            grad_qkv_w.astype(bf16).reshape(3 * per, s, D),
-            grad_out_w.astype(bf16)
-            .reshape(per, C, s, per, s)
-            .transpose(0, 2, 1, 3, 4)
-            .reshape(per, s, D),
-            grad_up_w.astype(bf16).reshape(hidden // B, s, D),
-            grad_down_w.astype(bf16).reshape(hidden // B, s, D),
-        ],
-        axis=0,
-    )
+    grad_groups = [
+        grad_qkv_w.reshape(3 * per, s, D),
+        grad_out_w.reshape(per, C, s, per, s).transpose(0, 2, 1, 3, 4).reshape(per, s, D),
+        grad_up_w.reshape(hidden // B, s, D),
+        grad_down_w.reshape(hidden // B, s, D),
+    ]
     if direct:
-        by_owner = grad_blocks.reshape(C, K, nb * s, D)
-        total = at(by_owner, c, 1).astype(f32)
+        reduced = jnp.concatenate([reduce_blocks(group) for group in grad_groups], axis=0)
+        reduced = reduced.reshape(C, K * nb, C, s // K // C, D)
+        arrived = [at(reduced, g)] + [hop(at(reduced, g ^ d), d) for d in range(1, C)]
+        arrived = jnp.stack(arrived).reshape(C, K, nb, C, s // K // C, D)
+        pieces = [at(arrived, c, 1)]
         for k in range(1, K):
-            total = total + cores(at(by_owner, (c + k) % K, 1), k).astype(f32)
-        parts = total.reshape(C, nb, C, s // C, D).transpose(2, 0, 1, 3, 4)
-        reduced = ring_scatter(parts).astype(bf16)
-        pieces = [at(reduced, g)]
-        for d in range(1, C):
-            pieces.append(hop(at(reduced, g ^ d), d))
-        pieces = jnp.stack(pieces)
-        ordered = jnp.stack([at(pieces, gg ^ g) for gg in range(C)], axis=1)
-        ordered = jnp.stack(ring_gather(ordered), axis=2)
-        ordered = ordered.reshape(nb, C, s, D)
-        grad_out = jnp.where(
-            is_o.reshape(-1, 1, 1), from_column_form(ordered), ordered.reshape(nb, B, D)
-        ).reshape(own_rows, D)
+            pieces.append(cores(at(arrived, (c + k) % K, 1), k))
+        grad_out, weights_out, first_out, second_out = update(
+            place, pieces, weight_rows, first_rows, second_rows, C, K, s, per, nb, bounds
+        )
     else:
         spread = lax.dynamic_update_slice(
-            jnp.zeros((blocks, C, s, D), bf16), grad_blocks[:, None], (0, g, 0, 0)
+            jnp.zeros((blocks, C, s, D), bf16),
+            jnp.concatenate(grad_groups, axis=0).astype(bf16)[:, None],
+            (0, g, 0, 0),
         )
         matrix = jnp.where(
             ((jnp.arange(blocks) >= first_o) & (jnp.arange(blocks) < last_o))[:, None, None],
@@ -323,9 +450,10 @@
             spread.reshape(blocks, B, D),
         ).reshape(total_rows, D)
         grad_out = lax.psum_scatter(matrix, "fsdp", scatter_dimension=0, tiled=True)
-        grad_out = lax.psum(grad_out, "ctx")
-    grad_out = grad_out.astype(f32)
-    weights_out, first_out, second_out = adam_update(weight_rows, grad_out, first_rows, second_rows)
+        grad_out = lax.psum(grad_out, "ctx").astype(f32)
+        weights_out, first_out, second_out = adam_update(
+            weight_rows, grad_out, first_rows, second_rows
+        )
     return (
         output.reshape(1, T, D),
         grad_inputs.astype(f32).reshape(1, T, D),

time: 504 us -> 506 us (level)
  starting transfers between devices: 68.7 us -> 124 us
  blocking collectives: 54.8 us -> 0 us
  Pallas kernels: 0 us -> 46.4 us
  local copies, waits for them, and re-layouts: 64.5 us -> 29.3 us
  other arithmetic: 55.4 us -> 23.8 us
  waiting for transfers between devices: 225 us -> 245 us
    psum x1 -> x0, blocking collectives: 54.8 us -> none  [local(): vector_total = lax.psum(vector_total, ('ctx', 'fsdp'))]
    pallas_call x0 -> x3, Pallas kernels: none -> 46.4 us  [the longest x1 21.1 us: update(): pl.pallas_call(lambda *refs: update_kernel(C, K, s, per, nb, bounds, *ref...]
    ppermute x10 -> x33, starting transfers between devices: 28.3 us -> 59.9 us  [the longest x24 37.3 us: along(): return lax.ppermute(array, 'ctx', [(i, i ^ e) for i in range(C)])]
    ppermute x30, starting transfers between devices: 40.3 us -> 63.4 us  [hop(): lax.ppermute(array, 'fsdp', [(i, K * (i // K ^ d) + i % K) for i in range...]
    sub x2 -> x1, other arithmetic: 20.3 us -> 0.71 us  [adam_update(): weights - learn_rate * (first_hat / (jnp.sqrt(second_hat) + adam_eps) + d...]
    ppermute x10 -> x33, waiting for transfers between devices: 124 us -> 144 us  [the longest x24 98.3 us: along(): return lax.ppermute(array, 'ctx', [(i, i ^ e) for i in range(C)])]
    dynamic_slice x11 -> x3, local copies, waits for them, and re-layouts: 14 us -> 1 us  [at(): return lax.dynamic_index_in_dim(array, index, axis, keepdims=False)]
    reshape x6 -> x2, local copies, waits for them, and re-layouts: 13.5 us -> 0.73 us  [local(): w_o = slices[first_o:last_o].reshape(per, s, C, per, s).transpose(0, 2, 1...]
  transfers between devices with their start and end apart: 42 -> 72, of which waited for: 26 -> 37; matrix products, arithmetic and copies ran while one was open for 6% -> 8% of each run, Pallas kernels for 0% -> 0%
where the time goes in v2:
time: 506 us; the launch traced here: 502 us
  waiting for transfers between devices  245 us (48%)
  starting transfers between devices  124 us (25%)
  Pallas kernels  46.4 us (9%)
  matrix products  30.9 us (6%)
  local copies, waits for them, and re-layouts  29.3 us (6%)
  other arithmetic  23.8 us (5%)
    ppermute x30, waiting for transfers between devices, hop(): lax.ppermute(array, 'fsdp', [(i, K * (i // K ^ d) + i % K) for i in range...  101 us
    ppermute x24, waiting for transfers between devices, along(): return lax.ppermute(array, 'ctx', [(i, i ^ e) for i in range(C)])  98.3 us
    ppermute x30, starting transfers between devices, hop(): lax.ppermute(array, 'fsdp', [(i, K * (i // K ^ d) + i % K) for i in range...  63.4 us
    ppermute x24, starting transfers between devices, along(): return lax.ppermute(array, 'ctx', [(i, i ^ e) for i in range(C)])  37.3 us
    pallas_call x1, Pallas kernels, update(): pl.pallas_call(lambda *refs: update_kernel(C, K, s, per, nb, bounds, *ref...  21.1 us
    pallas_call x1, Pallas kernels, unpack(): pl.pallas_call(lambda *refs: unpack_kernel(K, nb, *refs), out_shape=jax.S...  16.3 us
    ppermute x2, waiting for transfers between devices, swap(): return lax.ppermute(array, ('ctx', 'fsdp'), there)  15.8 us
    ppermute x5, waiting for transfers between devices, all_sum(): lax.ppermute(values, axis, [(i, i ^ step) for i in range(size)])  15.2 us
  transfers between devices with their start and end apart: 72, of which 37 were waited for; matrix products, arithmetic and copies ran while one was open for 8% of the time, Pallas kernels for 0%

profile of v2, /device:TPU:14, one launch (start us, length us, event | category | flops | bytes accessed | tf_op | source)
XLA Modules:
  0.0 501.7 jit_solution(1584224650352846542)
XLA Ops:
  1.3 8.9 %pack.1 = bf16[4,3,128,1024]{3,2,1,0:T(8,128)(2,1)} custom-call(s32[4]{0:T(128)} %pad_add_fusion.refs_0_, f32[1536,1024]{1,0:T(8,128)} %refs_5_.1), custom_call_target="tpu_custom_call" | custom-call | tf_op jit(solution)/shard_map/pack/pallas_call | solution.py:91
  17.3 4.5 collective-permute-start
  21.8 15.8 %collective-permute-done = bf16[128,1024]{1,0:T(8,128)(2,1)S(1)} collective-permute-done((bf16[128,1024]{1,0:T(8,128)(2,1)S(1)}, bf16[128,1024]{1,0:T(8,128)(2,1)S(1)}, u32[]{:S(2)}, u32[]{:S(2)}) %collective-permute-start) | collective-permute-done | bytes 262176 | tf_op jit(solution)/shard_map/ppermute | solution.py:232
  37.6 25.9 %collective-permute-start.2 = (bf16[128,1024]{1,0:T(8,128)(2,1)S(1)}, bf16[128,1024]{1,0:T(8,128)(2,1)S(1)}, u32[]{:S(2)}, u32[]{:S(2)}) collective-permute-start(bf16[128,1024]{1,0:T(8,128)(2,1)S(1)} %collective-permute-done), channel_id=1, source_target_pairs={{0,4},{1,5},{2,6},{3,7},{4,0},{5,1},{6,2},{7,3},{8,12},{9,13},{10,... | collective-permute-start | bytes 786440 | tf_op jit(solution)/shard_map/ppermute | solution.py:238
  71.7 6.5 %collective-permute-done.3 = bf16[128,1024]{1,0:T(8,128)(2,1)S(1)} collective-permute-done((bf16[128,1024]{1,0:T(8,128)(2,1)S(1)}, bf16[128,1024]{1,0:T(8,128)(2,1)S(1)}, u32[]{:S(2)}, u32[]{:S(2)}) %collective-permute-start.3) | collective-permute-done | bytes 262176 | tf_op jit(solution)/shard_map/ppermute | solution.py:238
  83.6 16.3 %unpack.1 = bf16[24,128,1024]{2,1,0:T(8,128)(2,1)} custom-call(s32[4]{0:T(128)} %pad_add_fusion.refs_0_, bf16[4,3,128,1024]{3,2,1,0:T(8,128)(2,1)} %pad_maximum_fusion.refs_1_, bf16[4,3,128,1024]{3,2,1,0:T(8,128)(2,1)} %pad_maximum_fusion.1.refs_2_), custom_call_target="tpu_custom_call" | custom-call | tf_op jit(solution)/shard_map/unpack/pallas_call | solution.py:120
  116.3 5.5 %collective-permute-done.13 = bf16[128,1024]{1,0:T(8,128)(2,1)S(1)} collective-permute-done((bf16[128,1024]{1,0:T(8,128)(2,1)}, bf16[128,1024]{1,0:T(8,128)(2,1)S(1)}, u32[]{:S(2)}, u32[]{:S(2)}) %collective-permute-start.13) | collective-permute-done | bytes 262176 | tf_op jit(solution)/shard_map/ppermute | solution.py:238
  121.8 4.1 collective-permute-done.12
  139.3 4.6 collective-permute-done.15
  152.5 4.4 collective-permute-start.21
  159.2 10.2 %collective-permute-done.18 = bf16[128,1024]{1,0:T(8,128)(2,1)S(1)} collective-permute-done((bf16[128,1024]{1,0:T(8,128)(2,1)S(1)}, bf16[128,1024]{1,0:T(8,128)(2,1)S(1)}, u32[]{:S(2)}, u32[]{:S(2)}) %collective-permute-start.18) | collective-permute-done | bytes 262176 | tf_op jit(solution)/shard_map/ppermute | solution.py:238
  172.3 5.6 %collective-permute-start.24 = (bf16[128,1024]{1,0:T(8,128)(2,1)S(1)}, bf16[128,1024]{1,0:T(8,128)(2,1)S(1)}, u32[]{:S(2)}, u32[]{:S(2)}) collective-permute-start(bf16[128,1024]{1,0:T(8,128)(2,1)S(1)} %convert_element_type.292), channel_id=1, source_target_pairs={{0,6},{1,7},{2,4},{3,5},{4,2},{5,3},{6,0},{7,1},{8,14},{9,15},{10,... | collective-permute-start | bytes 786440 | tf_op jit(solution)/shard_map/ppermute | solution.py:238
  178.6 6.6 %collective-permute-done.24 = bf16[128,1024]{1,0:T(8,128)(2,1)S(1)} collective-permute-done((bf16[128,1024]{1,0:T(8,128)(2,1)S(1)}, bf16[128,1024]{1,0:T(8,128)(2,1)S(1)}, u32[]{:S(2)}, u32[]{:S(2)}) %collective-permute-start.24) | collective-permute-done | bytes 262176 | tf_op jit(solution)/shard_map/ppermute | solution.py:238
  189.2 5.7 %fusion.108 = (f32[1024]{0:T(1024)}, bf16[512,1024]{1,0:T(8,128)(2,1)S(1)}) fusion(f32[512,1024]{1,0:T(8,128)} %get-tuple-element.96, f32[1024]{0:T(1024)S(1)} %bitcast.361, bf16[1024,1024]{1,0:T(8,128)(2,1)} %bitcast.301, bf16[128,1024]{1,0:T(8,128)(2,1)S(1)} %collective-permute-done.24, bf16[128,1024]{1,0:T(8,128)(2,1)S(1)} %collective-permute-done.23, ...), kind=kOutput, calls=%fused_computation.199 | convolution fusion | flops 1084226560 | bytes 6299648 | tf_op jit(solution)/shard_map/dot_general | solution.py:27
  206.5 4.4 collective-permute-done.26
  218.8 4.1 collective-permute-done.30
  222.9 4.4 collective-permute-done.29
  259.5 20.6 %collective-permute-done.59 = bf16[8,16,1024]{2,1,0:T(8,128)(2,1)S(1)} collective-permute-done((bf16[8,16,1024]{2,1,0:T(8,128)(2,1)S(1)}, bf16[8,16,1024]{2,1,0:T(8,128)(2,1)S(1)}, u32[]{:S(2)}, u32[]{:S(2)}) %collective-permute-start.59) | collective-permute-done | bytes 262176 | tf_op jit(solution)/shard_map/ppermute | solution.py:255
  291.0 5.9 %collective-permute-done.52 = bf16[8,16,1024]{2,1,0:T(8,128)(2,1)S(1)} collective-permute-done((bf16[8,16,1024]{2,1,0:T(8,128)(2,1)S(1)}, bf16[8,16,1024]{2,1,0:T(8,128)(2,1)S(1)}, u32[]{:S(2)}, u32[]{:S(2)}) %collective-permute-start.52) | collective-permute-done | bytes 262176 | tf_op jit(solution)/shard_map/ppermute | solution.py:255
  297.6 13.0 %collective-permute-done.51 = bf16[8,16,1024]{2,1,0:T(8,128)(2,1)S(1)} collective-permute-done((bf16[8,16,1024]{2,1,0:T(8,128)(2,1)S(1)}, bf16[8,16,1024]{2,1,0:T(8,128)(2,1)S(1)}, u32[]{:S(2)}, u32[]{:S(2)}) %collective-permute-start.51) | collective-permute-done | bytes 262176 | tf_op jit(solution)/shard_map/ppermute | solution.py:255
  317.0 15.0 %collective-permute-done.38 = bf16[6,16,1024]{2,1,0:T(8,128)(2,1)S(1)} collective-permute-done((bf16[6,16,1024]{2,1,0:T(8,128)(2,1)S(1)}, bf16[6,16,1024]{2,1,0:T(8,128)(2,1)S(1)}, u32[]{:S(2)}, u32[]{:S(2)}) %collective-permute-start.38) | collective-permute-done | bytes 196640 | tf_op jit(solution)/shard_map/ppermute | solution.py:255
  335.9 4.3 collective-permute-start.54
  340.3 10.8 %collective-permute-done.61 = bf16[8,16,1024]{2,1,0:T(8,128)(2,1)S(1)} collective-permute-done((bf16[8,16,1024]{2,1,0:T(8,128)(2,1)S(1)}, bf16[8,16,1024]{2,1,0:T(8,128)(2,1)S(1)}, u32[]{:S(2)}, u32[]{:S(2)}) %collective-permute-start.61) | collective-permute-done | bytes 262176 | tf_op jit(solution)/shard_map/ppermute | solution.py:255
  352.4 4.6 collective-permute-start.40
  357.0 10.2 %collective-permute-done.55 = bf16[8,16,1024]{2,1,0:T(8,128)(2,1)S(1)} collective-permute-done((bf16[8,16,1024]{2,1,0:T(8,128)(2,1)S(1)}, bf16[8,16,1024]{2,1,0:T(8,128)(2,1)S(1)}, u32[]{:S(2)}, u32[]{:S(2)}) %collective-permute-start.55) | collective-permute-done | bytes 262176 | tf_op jit(solution)/shard_map/ppermute | solution.py:255
  371.1 6.0 %collective-permute-done.41 = bf16[6,16,1024]{2,1,0:T(8,128)(2,1)S(1)} collective-permute-done((bf16[6,16,1024]{2,1,0:T(8,128)(2,1)S(1)}, bf16[6,16,1024]{2,1,0:T(8,128)(2,1)S(1)}, u32[]{:S(2)}, u32[]{:S(2)}) %collective-permute-start.41) | collective-permute-done | bytes 196640 | tf_op jit(solution)/shard_map/ppermute | solution.py:255
  386.0 17.9 %collective-permute-done.65 = bf16[6,4,16,1024]{3,2,1,0:T(8,128)(2,1)S(1)} collective-permute-done((bf16[6,4,16,1024]{3,2,1,0:T(8,128)(2,1)S(1)}, bf16[6,4,16,1024]{3,2,1,0:T(8,128)(2,1)S(1)}, u32[]{:S(2)}, u32[]{:S(2)}) %collective-permute-start.65) | collective-permute-done | bytes 786464 | tf_op jit(solution)/shard_map/ppermute | solution.py:238
  403.9 15.8 %collective-permute-done.64 = bf16[6,4,16,1024]{3,2,1,0:T(8,128)(2,1)S(1)} collective-permute-done((bf16[6,4,16,1024]{3,2,1,0:T(8,128)(2,1)S(1)}, bf16[6,4,16,1024]{3,2,1,0:T(8,128)(2,1)S(1)}, u32[]{:S(2)}, u32[]{:S(2)}) %collective-permute-start.64) | collective-permute-done | bytes 786464 | tf_op jit(solution)/shard_map/ppermute | solution.py:238
  434.0 7.4 %collective-permute-done.68 = f32[12,1024]{1,0:T(8,128)S(1)} collective-permute-done((f32[12,1024]{1,0:T(8,128)S(1)}, f32[12,1024]{1,0:T(8,128)S(1)}, u32[]{:S(2)}, u32[]{:S(2)}) %collective-permute-start.68) | collective-permute-done | bytes 49184 | tf_op jit(solution)/shard_map/ppermute | solution.py:261
  450.6 4.3 collective-permute-start.20
  461.1 11.8 %collective-permute-done.20 = bf16[128,1024]{1,0:T(8,128)(2,1)S(1)} collective-permute-done((bf16[128,1024]{1,0:T(8,128)(2,1)S(1)}, bf16[128,1024]{1,0:T(8,128)(2,1)S(1)}, u32[]{:S(2)}, u32[]{:S(2)}) %collective-permute-start.20) | collective-permute-done | bytes 262176 | tf_op jit(solution)/shard_map/ppermute | solution.py:235
  479.8 21.1 %update.1 = (f32[1536,1024]{1,0:T(8,128)}, f32[1536,1024]{1,0:T(8,128)}, f32[1536,1024]{1,0:T(8,128)}, f32[1536,1024]{1,0:T(8,128)}) custom-call(s32[4]{0:T(128)} %pad_add_fusion.refs_0_, bf16[4,3,4,16,1024]{4,3,2,1,0:T(8,128)(2,1)} %get-tuple-element.42.refs_1_.refs_3_, bf16[4,3,4,16,1024]{4,3,2,1,0:T(8,128)(2,1)} %copy-done.2, ...), custom_call_target="tpu_custom_call" | custom-call | tf_op jit(solution)/shard_map/update/pallas_call | solution.py:179
  (340 shorter events, 193.7 us)
Async XLA Ops:
  13.8 50.3 %collective-permute-start.6 = (bf16[3,128,1024]{2,1,0:T(8,128)(2,1)}, bf16[3,128,1024]{2,1,0:T(8,128)(2,1)}, u32[]{:S(2)}, u32[]{:S(2)}) collective-permute-start(bf16[3,128,1024]{2,1,0:T(8,128)(2,1)} %get-tuple-element.48), channel_id=1, source_target_pairs={{0,6},{1,7},{2,4},{3,5},{4,2},{5,3},{6,0},{7,1},{8,14},{9,15},{10,... | collective-permute-start | bytes 2359304 | tf_op jit(solution)/shard_map/ppermute | solution.py:238
  14.3 50.4 %collective-permute-start.5 = (bf16[3,128,1024]{2,1,0:T(8,128)(2,1)}, bf16[3,128,1024]{2,1,0:T(8,128)(2,1)}, u32[]{:S(2)}, u32[]{:S(2)}) collective-permute-start(bf16[3,128,1024]{2,1,0:T(8,128)(2,1)} %get-tuple-element.49), channel_id=1, source_target_pairs={{0,4},{1,5},{2,6},{3,7},{4,0},{5,1},{6,2},{7,3},{8,12},{9,13},{10,... | collective-permute-start | bytes 2359304 | tf_op jit(solution)/shard_map/ppermute | solution.py:238
  15.8 48.9 %collective-permute-start.4 = (bf16[3,128,1024]{2,1,0:T(8,128)(2,1)S(1)}, bf16[3,128,1024]{2,1,0:T(8,128)(2,1)}, u32[]{:S(2)}, u32[]{:S(2)}) collective-permute-start(bf16[3,128,1024]{2,1,0:T(8,128)(2,1)S(1)} %get-tuple-element.50), channel_id=1, source_target_pairs={{0,2},{1,3},{2,0},{3,1},{4,6},{5,7},{6,4},{7,5},{8,10},{9,11},{10,... | collective-permute-start | bytes 2359304 | tf_op jit(solution)/shard_map/ppermute | solution.py:238
  37.6 26.5 %collective-permute-start.1 = (bf16[128,1024]{1,0:T(8,128)(2,1)S(1)}, bf16[128,1024]{1,0:T(8,128)(2,1)S(1)}, u32[]{:S(2)}, u32[]{:S(2)}) collective-permute-start(bf16[128,1024]{1,0:T(8,128)(2,1)S(1)} %collective-permute-done), channel_id=1, source_target_pairs={{0,2},{1,3},{2,0},{3,1},{4,6},{5,7},{6,4},{7,5},{8,10},{9,11},{10,... | collective-permute-start | bytes 786440 | tf_op jit(solution)/shard_map/ppermute | solution.py:238
  37.6 31.1 %collective-permute-start.2 = (bf16[128,1024]{1,0:T(8,128)(2,1)S(1)}, bf16[128,1024]{1,0:T(8,128)(2,1)S(1)}, u32[]{:S(2)}, u32[]{:S(2)}) collective-permute-start(bf16[128,1024]{1,0:T(8,128)(2,1)S(1)} %collective-permute-done), channel_id=1, source_target_pairs={{0,4},{1,5},{2,6},{3,7},{4,0},{5,1},{6,2},{7,3},{8,12},{9,13},{10,... | collective-permute-start | bytes 786440 | tf_op jit(solution)/shard_map/ppermute | solution.py:238
  202.5 49.3 %collective-permute-start.56 = (bf16[8,64,1024]{2,1,0:T(8,128)(2,1)}, bf16[8,64,1024]{2,1,0:T(8,128)(2,1)}, u32[]{:S(2)}, u32[]{:S(2)}) collective-permute-start(bf16[8,64,1024]{2,1,0:T(8,128)(2,1)} %fusion.9), channel_id=1, source_target_pairs={{0,1},{1,0},{2,3},{3,2},{4,5},{5,4},{6,7},{7,6},{8,9},{9,8},{10,11... | collective-permute-start | bytes 3145736 | tf_op jit(solution)/shard_map/ppermute | solution.py:252
  218.8 36.7 %collective-permute-start.49 = (bf16[8,64,1024]{2,1,0:T(8,128)(2,1)}, bf16[8,64,1024]{2,1,0:T(8,128)(2,1)}, u32[]{:S(2)}, u32[]{:S(2)}) collective-permute-start(bf16[8,64,1024]{2,1,0:T(8,128)(2,1)} %fusion.8), channel_id=1, source_target_pairs={{0,1},{1,0},{2,3},{3,2},{4,5},{5,4},{6,7},{7,6},{8,9},{9,8},{10,11... | collective-permute-start | bytes 3145736 | tf_op jit(solution)/shard_map/ppermute | solution.py:252
  249.0 38.5 %collective-permute-start.48 = (bf16[2,16,1024]{2,1,0:T(8,128)(2,1)S(1)}, bf16[2,16,1024]{2,1,0:T(8,128)(2,1)S(1)}, u32[]{:S(2)}, u32[]{:S(2)}) collective-permute-start(bf16[2,16,1024]{2,1,0:T(8,128)(2,1)S(1)} %fusion.73), channel_id=1, source_target_pairs={{0,24},{8,16},{16,8},{24,0},{1,25},{9,17},{17,9},{25,1},{2,26},{10... | collective-permute-start | bytes 196616 | tf_op jit(solution)/shard_map/ppermute | solution.py:255
  249.7 40.0 %collective-permute-start.47 = (bf16[2,16,1024]{2,1,0:T(8,128)(2,1)S(1)}, bf16[2,16,1024]{2,1,0:T(8,128)(2,1)S(1)}, u32[]{:S(2)}, u32[]{:S(2)}) collective-permute-start(bf16[2,16,1024]{2,1,0:T(8,128)(2,1)S(1)} %fusion.73), channel_id=1, source_target_pairs={{0,16},{8,24},{16,0},{24,8},{1,17},{9,25},{17,1},{25,9},{2,18},{10... | collective-permute-start | bytes 196616 | tf_op jit(solution)/shard_map/ppermute | solution.py:255
  253.8 26.3 %collective-permute-start.59 = (bf16[8,16,1024]{2,1,0:T(8,128)(2,1)S(1)}, bf16[8,16,1024]{2,1,0:T(8,128)(2,1)S(1)}, u32[]{:S(2)}, u32[]{:S(2)}) collective-permute-start(bf16[8,16,1024]{2,1,0:T(8,128)(2,1)S(1)} %get-tuple-element.57), channel_id=1, source_target_pairs={{0,24},{8,16},{16,8},{24,0},{1,25},{9,17},{17,9},{25,1},{2,26},{10... | collective-permute-start | bytes 786440 | tf_op jit(solution)/shard_map/ppermute | solution.py:255
  255.5 28.4 %collective-permute-start.58 = (bf16[8,16,1024]{2,1,0:T(8,128)(2,1)S(1)}, bf16[8,16,1024]{2,1,0:T(8,128)(2,1)S(1)}, u32[]{:S(2)}, u32[]{:S(2)}) collective-permute-start(bf16[8,16,1024]{2,1,0:T(8,128)(2,1)S(1)} %get-tuple-element.56), channel_id=1, source_target_pairs={{0,16},{8,24},{16,0},{24,8},{1,17},{9,25},{17,1},{25,9},{2,18},{10... | collective-permute-start | bytes 786440 | tf_op jit(solution)/shard_map/ppermute | solution.py:255
  258.8 28.5 %collective-permute-start.57 = (bf16[8,16,1024]{2,1,0:T(8,128)(2,1)S(1)}, bf16[8,16,1024]{2,1,0:T(8,128)(2,1)S(1)}, u32[]{:S(2)}, u32[]{:S(2)}) collective-permute-start(bf16[8,16,1024]{2,1,0:T(8,128)(2,1)S(1)} %get-tuple-element.55), channel_id=1, source_target_pairs={{0,8},{8,0},{16,24},{24,16},{1,9},{9,1},{17,25},{25,17},{2,10},{10... | collective-permute-start | bytes 786440 | tf_op jit(solution)/shard_map/ppermute | solution.py:255
  283.9 26.7 %collective-permute-start.51 = (bf16[8,16,1024]{2,1,0:T(8,128)(2,1)S(1)}, bf16[8,16,1024]{2,1,0:T(8,128)(2,1)S(1)}, u32[]{:S(2)}, u32[]{:S(2)}) collective-permute-start(bf16[8,16,1024]{2,1,0:T(8,128)(2,1)S(1)} %get-tuple-element.54), channel_id=1, source_target_pairs={{0,16},{8,24},{16,0},{24,8},{1,17},{9,25},{17,1},{25,9},{2,18},{10... | collective-permute-start | bytes 786440 | tf_op jit(solution)/shard_map/ppermute | solution.py:255
  287.3 26.7 %collective-permute-start.50 = (bf16[8,16,1024]{2,1,0:T(8,128)(2,1)S(1)}, bf16[8,16,1024]{2,1,0:T(8,128)(2,1)S(1)}, u32[]{:S(2)}, u32[]{:S(2)}) collective-permute-start(bf16[8,16,1024]{2,1,0:T(8,128)(2,1)S(1)} %get-tuple-element.52), channel_id=1, source_target_pairs={{0,8},{8,0},{16,24},{24,16},{1,9},{9,1},{17,25},{25,17},{2,10},{10... | collective-permute-start | bytes 786440 | tf_op jit(solution)/shard_map/ppermute | solution.py:255
  287.6 26.6 %collective-permute-start.46 = (bf16[2,16,1024]{2,1,0:T(8,128)(2,1)S(1)}, bf16[2,16,1024]{2,1,0:T(8,128)(2,1)S(1)}, u32[]{:S(2)}, u32[]{:S(2)}) collective-permute-start(bf16[2,16,1024]{2,1,0:T(8,128)(2,1)S(1)} %fusion.73), channel_id=1, source_target_pairs={{0,8},{8,0},{16,24},{24,16},{1,9},{9,1},{17,25},{25,17},{2,10},{10... | collective-permute-start | bytes 196616 | tf_op jit(solution)/shard_map/ppermute | solution.py:255
  289.7 50.5 %collective-permute-start.62 = (bf16[8,16,1024]{2,1,0:T(8,128)(2,1)S(1)}, bf16[8,16,1024]{2,1,0:T(8,128)(2,1)S(1)}, u32[]{:S(2)}, u32[]{:S(2)}) collective-permute-start(bf16[8,16,1024]{2,1,0:T(8,128)(2,1)S(1)} %fusion.40), channel_id=1, source_target_pairs={{0,24},{8,16},{16,8},{24,0},{1,25},{9,17},{17,9},{25,1},{2,26},{10... | collective-permute-start | bytes 786440 | tf_op jit(solution)/shard_map/ppermute | solution.py:255
  296.9 35.1 %collective-permute-start.38 = (bf16[6,16,1024]{2,1,0:T(8,128)(2,1)S(1)}, bf16[6,16,1024]{2,1,0:T(8,128)(2,1)S(1)}, u32[]{:S(2)}, u32[]{:S(2)}) collective-permute-start(bf16[6,16,1024]{2,1,0:T(8,128)(2,1)S(1)} %get-tuple-element.59), channel_id=1, source_target_pairs={{0,24},{8,16},{16,8},{24,0},{1,25},{9,17},{17,9},{25,1},{2,26},{10... | collective-permute-start | bytes 589832 | tf_op jit(solution)/shard_map/ppermute | solution.py:255
  310.6 23.9 %collective-permute-start.37 = (bf16[6,16,1024]{2,1,0:T(8,128)(2,1)S(1)}, bf16[6,16,1024]{2,1,0:T(8,128)(2,1)S(1)}, u32[]{:S(2)}, u32[]{:S(2)}) collective-permute-start(bf16[6,16,1024]{2,1,0:T(8,128)(2,1)S(1)} %get-tuple-element.60), channel_id=1, source_target_pairs={{0,16},{8,24},{16,0},{24,8},{1,17},{9,25},{17,1},{25,9},{2,18},{10... | collective-permute-start | bytes 589832 | tf_op jit(solution)/shard_map/ppermute | solution.py:255
  314.0 21.9 %collective-permute-start.36 = (bf16[6,16,1024]{2,1,0:T(8,128)(2,1)S(1)}, bf16[6,16,1024]{2,1,0:T(8,128)(2,1)S(1)}, u32[]{:S(2)}, u32[]{:S(2)}) collective-permute-start(bf16[6,16,1024]{2,1,0:T(8,128)(2,1)S(1)} %get-tuple-element.58), channel_id=1, source_target_pairs={{0,8},{8,0},{16,24},{24,16},{1,9},{9,1},{17,25},{25,17},{2,10},{10... | collective-permute-start | bytes 589832 | tf_op jit(solution)/shard_map/ppermute | solution.py:255
  314.2 36.9 %collective-permute-start.61 = (bf16[8,16,1024]{2,1,0:T(8,128)(2,1)S(1)}, bf16[8,16,1024]{2,1,0:T(8,128)(2,1)S(1)}, u32[]{:S(2)}, u32[]{:S(2)}) collective-permute-start(bf16[8,16,1024]{2,1,0:T(8,128)(2,1)S(1)} %fusion.40), channel_id=1, source_target_pairs={{0,16},{8,24},{16,0},{24,8},{1,17},{9,25},{17,1},{25,9},{2,18},{10... | collective-permute-start | bytes 786440 | tf_op jit(solution)/shard_map/ppermute | solution.py:255
  334.5 32.7 %collective-permute-start.55 = (bf16[8,16,1024]{2,1,0:T(8,128)(2,1)S(1)}, bf16[8,16,1024]{2,1,0:T(8,128)(2,1)S(1)}, u32[]{:S(2)}, u32[]{:S(2)}) collective-permute-start(bf16[8,16,1024]{2,1,0:T(8,128)(2,1)S(1)} %fusion.43), channel_id=1, source_target_pairs={{0,24},{8,16},{16,8},{24,0},{1,25},{9,17},{17,9},{25,1},{2,26},{10... | collective-permute-start | bytes 786440 | tf_op jit(solution)/shard_map/ppermute | solution.py:255
  335.9 35.2 %collective-permute-start.54 = (bf16[8,16,1024]{2,1,0:T(8,128)(2,1)S(1)}, bf16[8,16,1024]{2,1,0:T(8,128)(2,1)S(1)}, u32[]{:S(2)}, u32[]{:S(2)}) collective-permute-start(bf16[8,16,1024]{2,1,0:T(8,128)(2,1)S(1)} %fusion.43), channel_id=1, source_target_pairs={{0,16},{8,24},{16,0},{24,8},{1,17},{9,25},{17,1},{25,9},{2,18},{10... | collective-permute-start | bytes 786440 | tf_op jit(solution)/shard_map/ppermute | solution.py:255
  340.2 30.9 %collective-permute-start.53 = (bf16[8,16,1024]{2,1,0:T(8,128)(2,1)S(1)}, bf16[8,16,1024]{2,1,0:T(8,128)(2,1)S(1)}, u32[]{:S(2)}, u32[]{:S(2)}) collective-permute-start(bf16[8,16,1024]{2,1,0:T(8,128)(2,1)S(1)} %fusion.43), channel_id=1, source_target_pairs={{0,8},{8,0},{16,24},{24,16},{1,9},{9,1},{17,25},{25,17},{2,10},{10... | collective-permute-start | bytes 786440 | tf_op jit(solution)/shard_map/ppermute | solution.py:255
  351.1 26.0 %collective-permute-start.41 = (bf16[6,16,1024]{2,1,0:T(8,128)(2,1)S(1)}, bf16[6,16,1024]{2,1,0:T(8,128)(2,1)S(1)}, u32[]{:S(2)}, u32[]{:S(2)}) collective-permute-start(bf16[6,16,1024]{2,1,0:T(8,128)(2,1)S(1)} %fusion.53), channel_id=1, source_target_pairs={{0,24},{8,16},{16,8},{24,0},{1,25},{9,17},{17,9},{25,1},{2,26},{10... | collective-permute-start | bytes 589832 | tf_op jit(solution)/shard_map/ppermute | solution.py:255
  352.4 26.9 %collective-permute-start.40 = (bf16[6,16,1024]{2,1,0:T(8,128)(2,1)S(1)}, bf16[6,16,1024]{2,1,0:T(8,128)(2,1)}, u32[]{:S(2)}, u32[]{:S(2)}) collective-permute-start(bf16[6,16,1024]{2,1,0:T(8,128)(2,1)S(1)} %fusion.53), channel_id=1, source_target_pairs={{0,16},{8,24},{16,0},{24,8},{1,17},{9,25},{17,1},{25,9},{2,18},{10... | collective-permute-start | bytes 589832 | tf_op jit(solution)/shard_map/ppermute | solution.py:255
  383.9 35.8 %collective-permute-start.64 = (bf16[6,4,16,1024]{3,2,1,0:T(8,128)(2,1)S(1)}, bf16[6,4,16,1024]{3,2,1,0:T(8,128)(2,1)S(1)}, u32[]{:S(2)}, u32[]{:S(2)}) collective-permute-start(bf16[6,4,16,1024]{3,2,1,0:T(8,128)(2,1)S(1)} %get-tuple-element.45), channel_id=1, source_target_pairs={{0,4},{1,5},{2,6},{3,7},{4,0},{5,1},{6,2},{7,3},{8,12},{9,13},{10,... | collective-permute-start | bytes 2359304 | tf_op jit(solution)/shard_map/ppermute | solution.py:238
  384.5 35.1 %collective-permute-start.63 = (bf16[6,4,16,1024]{3,2,1,0:T(8,128)(2,1)S(1)}, bf16[6,4,16,1024]{3,2,1,0:T(8,128)(2,1)S(1)}, u32[]{:S(2)}, u32[]{:S(2)}) collective-permute-start(bf16[6,4,16,1024]{3,2,1,0:T(8,128)(2,1)S(1)} %get-tuple-element.46), channel_id=1, source_target_pairs={{0,2},{1,3},{2,0},{3,1},{4,6},{5,7},{6,4},{7,5},{8,10},{9,11},{10,... | collective-permute-start | bytes 2359304 | tf_op jit(solution)/shard_map/ppermute | solution.py:238
  422.2 56.5 %collective-permute-start.66 = (bf16[4,3,4,16,1024]{4,3,2,1,0:T(8,128)(2,1)}, bf16[4,3,4,16,1024]{4,3,2,1,0:T(8,128)(2,1)S(1)}, u32[]{:S(2)}, u32[]{:S(2)}) collective-permute-start(bf16[4,3,4,16,1024]{4,3,2,1,0:T(8,128)(2,1)} %get-tuple-element.41), channel_id=1, source_target_pairs={{0,1},{1,0},{2,3},{3,2},{4,5},{5,4},{6,7},{7,6},{8,9},{9,8},{10,11... | collective-permute-start | bytes 4718600 | tf_op jit(solution)/shard_map/ppermute | solution.py:252
  425.5 29.4 %collective-permute-start.33 = (bf16[128,1024]{1,0:T(8,128)(2,1)}, bf16[128,1024]{1,0:T(8,128)(2,1)S(1)}, u32[]{:S(2)}, u32[]{:S(2)}) collective-permute-start(bf16[128,1024]{1,0:T(8,128)(2,1)} %get-tuple-element.64), channel_id=1, source_target_pairs={{0,6},{1,7},{2,4},{3,5},{4,2},{5,3},{6,0},{7,1},{8,14},{9,15},{10,... | collective-permute-start | bytes 786440 | tf_op jit(solution)/shard_map/ppermute | solution.py:238
  426.9 30.1 %collective-permute-start.32 = (bf16[128,1024]{1,0:T(8,128)(2,1)}, bf16[128,1024]{1,0:T(8,128)(2,1)S(1)}, u32[]{:S(2)}, u32[]{:S(2)}) collective-permute-start(bf16[128,1024]{1,0:T(8,128)(2,1)} %get-tuple-element.65), channel_id=1, source_target_pairs={{0,4},{1,5},{2,6},{3,7},{4,0},{5,1},{6,2},{7,3},{8,12},{9,13},{10,... | collective-permute-start | bytes 786440 | tf_op jit(solution)/shard_map/ppermute | solution.py:238
  427.5 29.5 %collective-permute-start.31 = (bf16[128,1024]{1,0:T(8,128)(2,1)}, bf16[128,1024]{1,0:T(8,128)(2,1)}, u32[]{:S(2)}, u32[]{:S(2)}) collective-permute-start(bf16[128,1024]{1,0:T(8,128)(2,1)} %get-tuple-element.63), channel_id=1, source_target_pairs={{0,2},{1,3},{2,0},{3,1},{4,6},{5,7},{6,4},{7,5},{8,10},{9,11},{10,... | collective-permute-start | bytes 786440 | tf_op jit(solution)/shard_map/ppermute | solution.py:238
  450.6 22.3 %collective-permute-start.20 = (bf16[128,1024]{1,0:T(8,128)(2,1)S(1)}, bf16[128,1024]{1,0:T(8,128)(2,1)S(1)}, u32[]{:S(2)}, u32[]{:S(2)}) collective-permute-start(bf16[128,1024]{1,0:T(8,128)(2,1)S(1)} %copy-done.23), channel_id=1, source_target_pairs={{0,0},{1,1},{10,2},{11,3},{20,4},{21,5},{30,6},{31,7},{2,8},{3,9},... | collective-permute-start | bytes 786440 | tf_op jit(solution)/shard_map/ppermute | solution.py:235
  (98 other events, 1185.6 us)
